TPU v7x, 32 devices: a whole 2x2x4 slice. The times are simulated.
32 devices in a mesh: ctx: 4 (over y, x), fsdp: 8 (over z, core).
Axes of the slice: x: 2, y: 2, z: 4, core: 2. Of those that a mesh axis runs over, the one named last changes fastest.
Arguments:
- tokens: bfloat16 [8, 512, 2048], P('fsdp', 'ctx')
- attn_gain: float32 [2048], replicated, may hold values from 0.1 to 1.9
- query_gain: float32 [2048], replicated
- key_gain: float32 [2048], replicated
- w_query: bfloat16 [2048, 2048], P(('ctx', 'fsdp'))
- w_key: bfloat16 [2048, 2048], P(('ctx', 'fsdp'))
- w_value: bfloat16 [2048, 2048], P(('ctx', 'fsdp')), may hold values from -0.125 to 0.125
- output_weight: bfloat16 [2048, 2048], P(('ctx', 'fsdp')), may hold values from -2 to 2
- ffn_gain: float32 [2048], replicated, may hold values from 0.1 to 1.9
- router: bfloat16 [2048, 32], replicated
- experts: bfloat16 [2048, 32, 3072], P('ctx', 'fsdp')
- routes: int32 [8, 512, 8], P('fsdp', 'ctx'), may hold values from 0 to 31, all different within a row; in each aligned block of 128 rows (0 to 127, 128 to 255, ..., all dimensions but the last counted through in order) at most 34 rows name the same one
- cotangent: bfloat16 [8, 512, 2048], P('fsdp', 'ctx'), may hold values from -6 to 6
Outputs:
- output: bfloat16 [8, 512, 2048], P('fsdp', 'ctx')
- d_tokens: float32 [8, 512, 2048], P('fsdp', 'ctx')
- d_attn_gain: float32 [2048], replicated
- d_query_gain: float32 [2048], replicated
- d_key_gain: float32 [2048], replicated
- d_query: float32 [2048, 2048], P(('ctx', 'fsdp'))
- d_key: float32 [2048, 2048], P(('ctx', 'fsdp'))
- d_value: float32 [2048, 2048], P(('ctx', 'fsdp'))
- d_output: float32 [2048, 2048], P(('ctx', 'fsdp'))
- d_ffn_gain: float32 [2048], replicated
- d_router: float32 [2048, 32], replicated
- d_experts: float32 [2048, 32, 3072], P('ctx', 'fsdp')
Inputs may be any that keep to these rules, and one draw needn't show every extreme that they name: `routes`: each row names 8 different experts; in each aligned block of 128 rows (the rows of one device) no expert is named by more than 34 rows, a bound that some block reaches.
All inputs are finite; a program needn't handle non-finite values.
Results may differ from a plain program's by a relative error of at most 0.017.
Values may be sent and summed in bfloat16 or wider, within the bound.
No kernel may reach another device: no remote copies, remote signals or barrier semaphores. Data moves between devices by JAX's collectives and lax.ppermute only.
A program may use at most 512 MiB of HBM per device.

v0:
```python
import functools
import math

import jax
import jax.numpy as jnp
from jax import lax
from jax.experimental import pallas as pl
from jax.experimental.pallas import tpu as pltpu
from jax.sharding import PartitionSpec as P

HD = 128

epsilon = 1e-05
neg_large = -1e30
f32 = jnp.float32
bf16 = jnp.bfloat16
everyone = ("fsdp", "ctx")


def mm(a, b):
    return jnp.dot(a, b, preferred_element_type=f32)


def mm_nt(a, b):
    return lax.dot_general(a, b, (((1,), (1,)), ((), ())), preferred_element_type=f32)


def mm_tn(a, b):
    return lax.dot_general(a, b, (((0,), (0,)), ((), ())), preferred_element_type=f32)


def inv_rms(values):
    return lax.rsqrt(jnp.mean(values * values, -1, keepdims=True) + epsilon)


def norm_back(grad, values, scale, gain):
    weighted = grad * gain
    grad_values = scale * weighted - values * scale * scale * scale * jnp.mean(
        weighted * values, -1, keepdims=True
    )
    grad_gain = jnp.sum(grad * values * scale, axis=0)
    return (grad_values, grad_gain)


def rope_tables(positions, head_size):
    half_size = head_size // 2
    inverse_freq = jnp.exp(
        jnp.arange(half_size, dtype=f32) * (-2.0 * math.log(10000.0) / head_size)
    )
    angles = positions.astype(f32)[:, None] * inverse_freq[None, :]
    cosine = jnp.cos(angles)
    sine = jnp.sin(angles)
    return (jnp.concatenate([cosine, cosine], -1), jnp.concatenate([sine, sine], -1))


def from_peer(values, offset, total):
    return lax.ppermute(values, "ctx", [(i, i ^ offset) for i in range(total)])


def place_kernel(order, rows, block, place_ref, *refs):
    parts, whole, sems = refs[:-2], refs[-2], refs[-1]
    step = pl.program_id(0)
    copies = []
    for n, (j, half) in enumerate(order):
        first = ((place_ref[0] ^ j) * 2 + half) * rows + step * block
        first = pl.multiple_of(first, block)
        copies.append(
            pltpu.make_async_copy(parts[n], whole.at[pl.ds(first, block), :], sems.at[n])
        )
        copies[-1].start()
    for copy in copies:
        copy.wait()


def place_parts(place, order, parts):
    rows, width = parts[0].shape
    block = min(64, rows)
    steps = rows // block
    return pl.pallas_call(
        functools.partial(place_kernel, order, rows, block),
        grid_spec=pltpu.PrefetchScalarGridSpec(
            num_scalar_prefetch=1,
            grid=(steps,),
            in_specs=[pl.BlockSpec((block, width), lambda i, s: (i, 0))] * len(parts),
            out_specs=pl.BlockSpec(memory_space=pl.ANY),
            scratch_shapes=[pltpu.SemaphoreType.DMA((len(parts),))],
        ),
        out_shape=jax.ShapeDtypeStruct((len(parts) * rows, width), parts[0].dtype),
        compiler_params=pltpu.CompilerParams(vmem_limit_bytes=30 << 20),
        cost_estimate=pl.CostEstimate(
            flops=0, bytes_accessed=4 * len(parts) * rows * width, transcendentals=0
        ),
        name="place_parts",
    )(place, *parts)


def merge_kernel(steps, block, total, pieces, base, place_ref, *refs):
    parts, whole, held, sems = refs[: total * pieces], refs[-3], refs[-2], refs[-1]
    step = pl.program_id(0)
    slot = lax.rem(step, 2)

    def copy(at, side, m):
        rows = pl.ds(pl.multiple_of(base + at * block, block), block)
        return pltpu.make_async_copy(
            held.at[side, m], whole.at[rows, place_ref[0] ^ m, :], sems.at[side, m]
        )

    for m in range(total):

        @pl.when(step >= 2)
        def _():
            copy(step - 2, slot, m).wait()

        value = parts[m * pieces][...].astype(f32)
        for p in range(1, pieces):
            value = value + parts[m * pieces + p][...].astype(f32)
        held[slot, m] = value
        copy(step, slot, m).start()

    @pl.when(step == steps - 1)
    def _():
        for m in range(total):
            if steps >= 2:
                copy(step - 1, 1 - slot, m).wait()
            copy(step, slot, m).wait()


def merge_parts(place, parts, total, base, rows_total, whole=None):
    rows, width = parts[0].shape
    pieces = len(parts) // total
    block = min(64, rows)
    steps = rows // block
    more = [] if whole is None else [whole]
    return pl.pallas_call(
        functools.partial(merge_kernel, steps, block, total, pieces, base),
        grid_spec=pltpu.PrefetchScalarGridSpec(
            num_scalar_prefetch=1,
            grid=(steps,),
            in_specs=[pl.BlockSpec((block, width), lambda i, s: (i, 0))] * len(parts)
            + [pl.BlockSpec(memory_space=pl.ANY)] * len(more),
            out_specs=pl.BlockSpec(memory_space=pl.ANY),
            scratch_shapes=[
                pltpu.VMEM((2, total, block, width), f32),
                pltpu.SemaphoreType.DMA((2, total)),
            ],
        ),
        out_shape=jax.ShapeDtypeStruct((rows_total, total, width), f32),
        input_output_aliases={1 + len(parts): 0} if more else {},
        compiler_params=pltpu.CompilerParams(vmem_limit_bytes=30 << 20),
        cost_estimate=pl.CostEstimate(
            flops=0,
            bytes_accessed=2 * len(parts) * rows * width + 4 * total * rows * width,
            transcendentals=0,
        ),
        name="merge_parts",
    )(place, *parts, *more)


def gather_rows(values, total):
    return jnp.concatenate(
        [values] + [from_peer(values, j, total) for j in range(1, total)], 0
    )


def scatter_rows(partial, total):
    rows = partial.shape[0] // total
    result = partial[:rows]
    for j in range(1, total):
        piece = partial[j * rows : (j + 1) * rows].astype(bf16)
        result = result + from_peer(piece, j, total).astype(f32)
    return result


def sum_rows(values, total):
    count, width = values.shape
    bits = total.bit_length() - 1
    result = values
    for j in range(1, total):
        other = from_peer(values, j, total).reshape((count,) + (2,) * bits + (width // total,))
        other = jnp.flip(other, [1 + n for n in range(bits) if j >> (bits - 1 - n) & 1])
        result = result + other.reshape(count, width)
    return result


def dot_nn(a, b):
    return lax.dot_general(a, b, (((1,), (0,)), ((), ())), preferred_element_type=f32)


def expert_kernel(
    steps,
    mine_ref,
    rows_ref,
    cots_ref,
    router_ref,
    gate_w,
    up_w,
    down_w,
    back_ref,
    out_ref,
    grads_ref,
    ggate_ref,
    gup_ref,
    hidden_ref,
    total_out,
    total_back,
    weight,
):
    step = pl.program_id(0)
    mine = mine_ref[0]
    width = rows_ref.shape[1]
    expert_total = router_ref.shape[1]

    @pl.when(step == 0)
    def _():
        logits = dot_nn(rows_ref[...], router_ref[...])
        logits = jnp.exp(logits - jnp.max(logits, -1, keepdims=True))
        column = lax.broadcasted_iota(jnp.int32, logits.shape, 1)
        chosen = jnp.sum(jnp.where(column == mine, logits, 0.0), -1, keepdims=True)
        weight[...] = chosen / jnp.sum(logits, -1, keepdims=True)
        grads_ref[...] = (weight[...] * cots_ref[...].astype(f32)).astype(bf16)
        total_out[...] = jnp.zeros_like(total_out)
        total_back[...] = jnp.zeros_like(total_back)

    gate = dot_nn(rows_ref[...], gate_w[...])
    up = dot_nn(rows_ref[...], up_w[...])
    grad_hidden = dot_nn(grads_ref[...], down_w[...])
    sigma = jax.nn.sigmoid(gate)
    swish = gate * sigma
    hidden = (swish * up).astype(bf16)
    grad_gate = (grad_hidden * up * sigma * (1.0 + gate * (1.0 - sigma))).astype(bf16)
    grad_up = (grad_hidden * swish).astype(bf16)
    hidden_ref[...] = hidden
    ggate_ref[...] = grad_gate
    gup_ref[...] = grad_up
    total_out[...] += mm_nt(hidden, down_w[...])
    total_back[...] += mm_nt(grad_gate, gate_w[...]) + mm_nt(grad_up, up_w[...])

    @pl.when(step == steps - 1)
    def _():
        result = total_out[...].astype(bf16).astype(f32)
        out_ref[...] = (weight[...] * result).astype(bf16)
        grad_weight = jnp.sum(cots_ref[...].astype(f32) * result, -1, keepdims=True)
        high = grad_weight.astype(bf16).astype(f32)
        low = grad_weight - high
        back_ref[:, :width] = total_back[...].astype(bf16)
        extra = back_ref.shape[1] - width
        column = lax.broadcasted_iota(jnp.int32, (rows_ref.shape[0], extra), 1)
        side = jnp.where(column == mine, high, 0.0) + jnp.where(
            column == expert_total + mine, low, 0.0
        )
        back_ref[:, width:] = side.astype(bf16)


def run_expert(mine, rows, cots, router, expert, extra):
    count, width = rows.shape
    ff = expert.shape[1] // 3
    block = min(256, ff)
    steps = ff // block
    whole = pl.BlockSpec((count, width), lambda i, s: (0, 0))
    part = pl.BlockSpec((count, block), lambda i, s: (0, i))
    return pl.pallas_call(
        functools.partial(expert_kernel, steps),
        grid_spec=pltpu.PrefetchScalarGridSpec(
            num_scalar_prefetch=1,
            grid=(steps,),
            in_specs=[
                whole,
                whole,
                pl.BlockSpec(router.shape, lambda i, s: (0, 0)),
                pl.BlockSpec((width, block), lambda i, s: (0, i)),
                pl.BlockSpec((width, block), lambda i, s: (0, steps + i)),
                pl.BlockSpec((width, block), lambda i, s: (0, 2 * steps + i)),
            ],
            out_specs=[
                pl.BlockSpec((count, width + extra), lambda i, s: (0, 0)),
                whole,
                whole,
                part,
                part,
                part,
            ],
            scratch_shapes=[
                pltpu.VMEM((count, width), f32),
                pltpu.VMEM((count, width), f32),
                pltpu.VMEM((count, 1), f32),
            ],
        ),
        out_shape=[
            jax.ShapeDtypeStruct((count, width + extra), bf16),
            jax.ShapeDtypeStruct((count, width), bf16),
            jax.ShapeDtypeStruct((count, width), bf16),
            jax.ShapeDtypeStruct((count, ff), bf16),
            jax.ShapeDtypeStruct((count, ff), bf16),
            jax.ShapeDtypeStruct((count, ff), bf16),
        ],
        compiler_params=pltpu.CompilerParams(vmem_limit_bytes=48 << 20),
        cost_estimate=pl.CostEstimate(
            flops=12 * count * width * ff,
            bytes_accessed=6 * width * ff + 10 * count * width,
            transcendentals=count * ff,
        ),
        name="expert",
    )(mine, rows, cots, router, expert, expert, expert)


def weight_kernel(groups, steps, place_ref, *refs):
    step = pl.program_id(0)

    def total(left, right):
        result = mm_tn(refs[left][...], refs[right][...])
        for g in range(1, groups):
            result = result + mm_tn(refs[5 * g + left][...], refs[5 * g + right][...])
        half = refs[-1].shape[0]
        refs[-2][...] = result[:half].astype(bf16)
        refs[-1][...] = result[half:].astype(bf16)

    @pl.when(step < steps)
    def _():
        total(0, 2)

    @pl.when((step >= steps) & (step < 2 * steps))
    def _():
        total(0, 3)

    @pl.when(step >= 2 * steps)
    def _():
        total(1, 4)


def weight_grad(place, groups, columns):
    count, _ = groups[0][0].shape
    ff = groups[0][2].shape[1]
    block = min(512, ff)
    steps = ff // block
    side = pl.BlockSpec((count, columns), lambda i, s: (0, s[0]))

    def part(first):
        return pl.BlockSpec(
            (count, block),
            lambda i, s: (0, jnp.clip(i - first * steps, 0, steps - 1)),
        )

    return pl.pallas_call(
        functools.partial(weight_kernel, len(groups), steps),
        grid_spec=pltpu.PrefetchScalarGridSpec(
            num_scalar_prefetch=1,
            grid=(3 * steps,),
            in_specs=[side, side, part(0), part(1), part(2)] * len(groups),
            out_specs=[pl.BlockSpec((columns // 2, block), lambda i, s: (0, i))] * 2,
        ),
        out_shape=[jax.ShapeDtypeStruct((columns // 2, 3 * ff), bf16)] * 2,
        compiler_params=pltpu.CompilerParams(vmem_limit_bytes=48 << 20),
        cost_estimate=pl.CostEstimate(
            flops=6 * len(groups) * count * columns * ff,
            bytes_accessed=6 * columns * ff + 10 * len(groups) * count * ff,
            transcendentals=0,
        ),
        name="weight_grad",
    )(place, *[a for group in groups for a in group])


def collect_kernel(total, *refs):
    result = dot_nn(refs[0][...], refs[total][...])
    for j in range(1, total):
        result = result + dot_nn(refs[j][...], refs[total + j][...])
    refs[-1][...] = result.astype(bf16)


def collect_rows(places, parts):
    tokens = places[0].shape[0]
    rows, width = parts[0].shape
    block = 512 if width % 512 == 0 else 768
    return pl.pallas_call(
        functools.partial(collect_kernel, len(parts)),
        grid=(pl.cdiv(width, block),),
        in_specs=[pl.BlockSpec((tokens, rows), lambda i: (0, 0))] * len(parts)
        + [pl.BlockSpec((rows, block), lambda i: (0, i))] * len(parts),
        out_specs=pl.BlockSpec((tokens, block), lambda i: (0, i)),
        out_shape=jax.ShapeDtypeStruct((tokens, width), bf16),
        compiler_params=pltpu.CompilerParams(vmem_limit_bytes=48 << 20),
        cost_estimate=pl.CostEstimate(
            flops=2 * len(parts) * tokens * rows * width,
            bytes_accessed=2 * len(parts) * rows * (width + tokens) + 2 * tokens * width,
            transcendentals=0,
        ),
        name="collect_rows",
    )(*places, *parts)


def turn(values, cosine, sine):
    return values * cosine + pltpu.roll(values, HD // 2, 1) * sine


def head_forward(raw_q, raw_k, scale, gains, cosine, sine, row_pos, col_pos):
    query = turn(raw_q * scale[:, 0:1] * gains[0:1, :], cosine, sine).astype(bf16)
    key = turn(raw_k * scale[:, 1:2] * gains[1:2, :], cosine, sine).astype(bf16)
    scores = mm_nt(query, key) * (1.0 / math.sqrt(HD))
    scores = jnp.where(col_pos <= row_pos, scores, neg_large)
    weights = jnp.exp(scores - jnp.max(scores, -1, keepdims=True))
    return query, key, weights / jnp.sum(weights, -1, keepdims=True)


def attend_kernel(q_ref, k_ref, v_ref, scale_ref, gain_ref, cos_ref, sin_ref, rp, cp, out_ref):
    _, _, probs = head_forward(
        q_ref[...],
        k_ref[...],
        scale_ref[...],
        gain_ref[...],
        cos_ref[...],
        sin_ref[...],
        rp[...],
        cp[...],
    )
    out_ref[...] = dot_nn(probs.astype(bf16), v_ref[...].astype(bf16)).astype(bf16)


def attend_back_kernel(
    q_ref,
    k_ref,
    v_ref,
    scale_ref,
    gain_ref,
    cos_ref,
    sin_ref,
    rp,
    cp,
    grad_ref,
    yq_ref,
    yk_ref,
    gv_ref,
    dots_ref,
    gains_ref,
):
    raw_q = q_ref[...]
    raw_k = k_ref[...]
    scale = scale_ref[...]
    gains = gain_ref[...]
    query, key, probs = head_forward(
        raw_q, raw_k, scale, gains, cos_ref[...], sin_ref[...], rp[...], cp[...]
    )
    grad = grad_ref[...]
    grad_prob = mm_nt(grad, v_ref[...].astype(bf16))
    delta = jnp.sum(probs * grad_prob, -1, keepdims=True)
    grad_scores = (probs * (grad_prob - delta)).astype(bf16)
    gv_ref[...] = mm_tn(probs.astype(bf16), grad).astype(bf16)
    soft = 1.0 / math.sqrt(HD)
    back_sine = -sin_ref[...]
    grad_q = turn(dot_nn(grad_scores, key) * soft, cos_ref[...], back_sine)
    grad_k = turn(mm_tn(grad_scores, query) * soft, cos_ref[...], back_sine)
    yq_ref[...] = grad_q
    yk_ref[...] = grad_k
    part_q = grad_q * raw_q
    part_k = grad_k * raw_k
    gains_ref[0:1, :] = jnp.sum(part_q * scale[:, 0:1], 0, keepdims=True)
    gains_ref[1:2, :] = jnp.sum(part_k * scale[:, 1:2], 0, keepdims=True)
    dot_q = jnp.sum(part_q * gains[0:1, :], -1, keepdims=True)
    dot_k = jnp.sum(part_k * gains[1:2, :], -1, keepdims=True)

    @pl.when(pl.program_id(0) == 0)
    def _():
        dots_ref[...] = jnp.zeros_like(dots_ref)

    column = lax.broadcasted_iota(jnp.int32, dots_ref.shape, 1)
    dots_ref[...] += jnp.where(column == 0, dot_q, dot_k)


def head_specs(seq, heads):
    one = pl.BlockSpec((seq, HD), lambda h: (0, h))
    key = pl.BlockSpec((seq, HD), lambda h: (0, heads + h))
    value = pl.BlockSpec((seq, HD), lambda h: (0, 2 * heads + h))

    def fixed(shape):
        return pl.BlockSpec(shape, lambda h: (0, 0))

    specs = [
        one,
        key,
        value,
        fixed((seq, 2)),
        pl.BlockSpec((2, HD), lambda h: (0, h)),
        fixed((seq, HD)),
        fixed((seq, HD)),
        fixed((seq, 1)),
        fixed((1, seq)),
    ]
    return one, specs


def attend(raw_qkv, tables):
    seq = raw_qkv.shape[0]
    width = raw_qkv.shape[1] // 3
    heads = width // HD
    one, specs = head_specs(seq, heads)
    return pl.pallas_call(
        attend_kernel,
        grid=(heads,),
        in_specs=specs,
        out_specs=one,
        out_shape=jax.ShapeDtypeStruct((seq, width), bf16),
        compiler_params=pltpu.CompilerParams(vmem_limit_bytes=48 << 20),
        cost_estimate=pl.CostEstimate(
            flops=4 * seq * seq * width,
            bytes_accessed=12 * seq * width,
            transcendentals=seq * seq * heads,
        ),
        name="attend",
    )(raw_qkv, raw_qkv, raw_qkv, *tables)


def attend_back(raw_qkv, tables, grad):
    seq, width = grad.shape
    heads = width // HD
    one, specs = head_specs(seq, heads)
    return pl.pallas_call(
        attend_back_kernel,
        grid=(heads,),
        in_specs=specs + [one],
        out_specs=[
            one,
            one,
            one,
            pl.BlockSpec((seq, 2), lambda h: (0, 0)),
            pl.BlockSpec((2, HD), lambda h: (0, h)),
        ],
        out_shape=[
            jax.ShapeDtypeStruct((seq, width), f32),
            jax.ShapeDtypeStruct((seq, width), f32),
            jax.ShapeDtypeStruct((seq, width), bf16),
            jax.ShapeDtypeStruct((seq, 2), f32),
            jax.ShapeDtypeStruct((2, width), f32),
        ],
        compiler_params=pltpu.CompilerParams(vmem_limit_bytes=56 << 20),
        cost_estimate=pl.CostEstimate(
            flops=12 * seq * seq * width,
            bytes_accessed=24 * seq * width,
            transcendentals=seq * seq * heads,
        ),
        name="attend_back",
    )(raw_qkv, raw_qkv, raw_qkv, *tables, grad)


def layer(
    tokens,
    attn_gain,
    query_gain,
    key_gain,
    w_query,
    w_key,
    w_value,
    output_weight,
    ffn_gain,
    router,
    experts,
    routes,
    cotangent,
):
    row_total = tokens.shape[1]
    half_rows = row_total // 2
    model_width = tokens.shape[2]
    expert_total = router.shape[1]
    slice_rows = experts.shape[0]
    local_experts = experts.shape[1]
    top_count = routes.shape[2]
    ff = experts.shape[2] // 3
    C = lax.axis_size("ctx")
    F = lax.axis_size("fsdp")
    devices = C * F
    W = model_width // C
    seq = C * row_total
    shard = w_query.shape[0]
    pieces = C // local_experts
    cap_unit = 16 * expert_total * pieces
    piece_cap = (17 * row_total * top_count + cap_unit - 1) // cap_unit
    me = lax.axis_index("ctx")
    row = lax.axis_index("fsdp")
    my_expert = row * local_experts + me // pieces
    my_column = me * W

    tokens_low = tokens.reshape(row_total, model_width)
    tokens_seq = gather_rows(tokens_low, C)
    route_ids = routes.reshape(row_total, top_count)
    column_ids = lax.all_gather(route_ids, "fsdp", axis=0, tiled=True)

    def by_column(weight):
        return jnp.swapaxes(weight.reshape(shard, C, W), 0, 1)

    w_cols = lax.all_to_all(
        jnp.concatenate([by_column(w_query), by_column(w_key), by_column(w_value)], 2),
        "ctx",
        split_axis=0,
        concat_axis=0,
        tiled=True,
    )
    w_qkv = lax.all_gather(w_cols, "fsdp", axis=1, tiled=True).reshape(model_width, 3 * W)
    w_o = lax.all_gather(output_weight, "fsdp", axis=0, tiled=True)

    by_expert = lax.optimization_barrier(
        jnp.swapaxes(lax.optimization_barrier(experts), 0, 1)
    )
    half = slice_rows // 2
    own = []
    order = []
    for j in range(C):
        for part in range(2):
            piece = lax.dynamic_slice(
                by_expert, ((me ^ j) // pieces, part * half, 0), (1, half, 3 * ff)
            ).reshape(half, 3 * ff)
            order.append((j, part))
            if j == 0:
                own.append(piece)
            else:
                own.append(from_peer(piece, j, C))
    expert = place_parts(me.reshape(1), order, own)

    column_rows = F * row_total
    member = jnp.sum(
        (column_ids[:, :, None] == jnp.arange(expert_total, dtype=jnp.int32)).astype(f32), 1
    )
    order = jnp.arange(row_total, dtype=jnp.int32)
    earlier = jnp.einsum(
        "ts,fse->fte",
        (order[None, :] < order[:, None]).astype(bf16),
        member.astype(bf16).reshape(F, row_total, expert_total),
        preferred_element_type=f32,
    ).reshape(column_rows, expert_total)
    marked = jnp.where(member > 0.5, earlier, -1.0).T
    group_rows = F * piece_cap
    group_ids = jnp.arange(group_rows, dtype=jnp.int32)
    token_block = jnp.arange(column_rows, dtype=jnp.int32) // row_total
    same_block = (group_ids // piece_cap)[:, None] == token_block[None, :]
    selects = []
    places = []
    for j in range(C):
        target = me ^ j
        mark = lax.dynamic_slice_in_dim(marked, row * local_experts + target // pieces, 1, 0)
        slot = (target % pieces) * piece_cap + group_ids % piece_cap
        slot = slot.astype(f32)
        selects.append(((mark == slot[:, None]) & same_block).astype(bf16))
        places.append(((mark.T == slot[None, :]) & same_block.T).astype(bf16))

    def exchange(parts):
        result = []
        for j in range(C):
            if j == 0:
                result.append(parts[j])
            else:
                result.append(from_peer(parts[j], j, C))
        return result

    def deliver(values):
        return exchange([mm(select, values).astype(bf16) for select in selects])

    def collect(parts):
        return collect_rows(places, parts)

    cot_low = cotangent.reshape(row_total, model_width)
    cot_column = lax.all_gather(cot_low, "fsdp", axis=0, tiled=True)
    cot_rows = deliver(cot_column)

    place = me ^ jnp.arange(C, dtype=jnp.int32)
    within = jnp.arange(half_rows, dtype=jnp.int32)
    positions = jnp.concatenate(
        [
            place[:, None] * half_rows + within,
            (2 * C - 1 - place)[:, None] * half_rows + within,
        ],
        1,
    ).reshape(seq)
    cosine, sine = rope_tables(positions, HD)
    inputs_seq = tokens_seq.astype(f32)
    scale_one = inv_rms(inputs_seq)
    normed = (inputs_seq * scale_one * attn_gain).astype(bf16)
    gains = lax.dynamic_slice_in_dim(jnp.stack([query_gain, key_gain]), my_column, W, 1)
    w_qkv, selects, places = lax.optimization_barrier((w_qkv, selects, places))
    raw_qkv = mm(normed, w_qkv)
    raw_q = raw_qkv[:, :W]
    raw_k = raw_qkv[:, W : 2 * W]
    squares = sum_rows(jnp.stack([jnp.sum(raw_q * raw_q, -1), jnp.sum(raw_k * raw_k, -1)]), C)
    scales = lax.rsqrt(squares / model_width + epsilon).T
    signed_sine = jnp.where(jnp.arange(HD) < HD // 2, -1.0, 1.0) * sine
    tables = (
        scales,
        gains,
        cosine,
        signed_sine,
        positions.reshape(seq, 1),
        positions.reshape(1, seq),
    )
    attended = attend(raw_qkv, tables)
    inputs = tokens_low.astype(f32)
    hidden_one = inputs + scatter_rows(mm(attended, w_o), C)

    scale_two = inv_rms(hidden_one)
    ffn_in = (hidden_one * scale_two * ffn_gain).astype(bf16)
    probs = jax.nn.softmax(mm(ffn_in, router), -1)
    ffn_column = lax.all_gather(ffn_in, "fsdp", axis=0, tiled=True)
    expert_in = deliver(ffn_column)
    extra = -(-2 * expert_total // 128) * 128
    done = []
    mine = my_expert.reshape(1)
    for j in range(C):
        result = run_expert(mine, expert_in[j], cot_rows[j], router, expert, extra)
        if j == 0:
            result, mine = lax.optimization_barrier((result, mine))
        done.append(result)
    back = collect(exchange([d[0] for d in done]))
    back = lax.psum_scatter(back, "fsdp", scatter_dimension=0, tiled=True).astype(f32)
    groups = [(expert_in[j], done[j][2], done[j][3], done[j][4], done[j][5]) for j in range(C)]
    d_own = []
    for j in range(C):
        d_own.append(weight_grad((me ^ j).reshape(1), groups, slice_rows))
    d_experts = None
    for part in range(2):
        pieces_here = []
        for j in range(C):
            if j == 0:
                pieces_here.append(d_own[j][part])
            else:
                pieces_here.append(from_peer(d_own[j][part], j, C))
        d_experts = merge_parts(
            (me // pieces).reshape(1),
            pieces_here,
            local_experts,
            part * half,
            slice_rows,
            d_experts,
        )
    mixed = collect(exchange([d[1] for d in done]))
    mixed = lax.psum_scatter(mixed, "fsdp", scatter_dimension=0, tiled=True).astype(f32)

    grad_probs = (
        back[:, model_width : model_width + expert_total]
        + back[:, model_width + expert_total : model_width + 2 * expert_total]
    )
    grad_logits = (probs * (grad_probs - jnp.sum(probs * grad_probs, -1, keepdims=True))).astype(
        bf16
    )
    grad_ffn = back[:, :model_width] + mm_nt(grad_logits, router)
    grad_router = mm_tn(grad_logits, ffn_in)
    grad_hidden_one, grad_ffn_gain = norm_back(grad_ffn, hidden_one, scale_two, ffn_gain)
    grad_hidden_one = grad_hidden_one + cot_low.astype(f32)
    router_slice = jnp.sum(
        lax.all_to_all(grad_router.reshape(devices, -1, 128), everyone, 0, 0, tiled=True), 0
    )

    branch_seq = gather_rows(grad_hidden_one.astype(bf16), C)
    d_output = mm_tn(attended, branch_seq).astype(bf16)
    grad_att = mm_nt(branch_seq, w_o).astype(bf16)
    grad_att, d_output = lax.optimization_barrier((grad_att, d_output))
    d_output = lax.psum_scatter(
        d_output, "fsdp", scatter_dimension=0, tiled=True
    ).astype(f32)
    grad_q_n, grad_k_n, grad_value, dots, gain_grads = attend_back(
        raw_qkv, tables, grad_att
    )
    dots = sum_rows(dots.T, C)
    dots = dots / model_width
    late_hidden, _ = lax.optimization_barrier((hidden_one, dots))
    output = (late_hidden + mixed).astype(bf16).reshape(1, row_total, model_width)
    scale_q = scales[:, 0:1]
    scale_k = scales[:, 1:2]
    grad_q = (
        scale_q * grad_q_n * gains[0]
        - raw_qkv[:, :W] * scale_q * scale_q * scale_q * dots[0][:, None]
    ).astype(bf16)
    grad_k = (
        scale_k * grad_k_n * gains[1]
        - raw_qkv[:, W : 2 * W] * scale_k * scale_k * scale_k * dots[1][:, None]
    ).astype(bf16)
    grad_qkv = jnp.concatenate([grad_q, grad_k, grad_value], 1)
    d_cols = lax.psum_scatter(
        mm_tn(normed, grad_qkv).astype(bf16).reshape(C, F * shard, 3 * W),
        "fsdp",
        scatter_dimension=1,
        tiled=True,
    )
    d_cols = lax.all_to_all(d_cols, "ctx", 0, 0, tiled=True).reshape(C, shard, 3, W)
    d_qkv = [
        jnp.swapaxes(d_cols[:, :, n], 0, 1).reshape(shard, model_width).astype(f32)
        for n in range(3)
    ]

    grad_normed = scatter_rows(mm_nt(grad_qkv, w_qkv), C)
    grad_inputs, grad_attn_gain = norm_back(grad_normed, inputs, scale_one[:row_total], attn_gain)
    grad_inputs = grad_inputs + grad_hidden_one

    vector = jnp.concatenate(
        [
            grad_attn_gain,
            grad_ffn_gain,
            gain_grads[0],
            gain_grads[1],
            router_slice.reshape(-1),
        ]
    ).reshape(1, -1, 128)
    everything = lax.all_to_all(
        jnp.broadcast_to(vector, (devices,) + vector.shape[1:]), everyone, 0, 0, tiled=True
    ).reshape(devices, -1)
    d_attn_gain = jnp.sum(everything[:, :model_width], 0)
    d_ffn_gain = jnp.sum(everything[:, model_width : 2 * model_width], 0)
    by_place = jnp.sum(
        everything[:, 2 * model_width : 2 * model_width + 2 * W].reshape(F, C, 2, W), 0
    )
    d_query_gain = by_place[:, 0].reshape(model_width)
    d_key_gain = by_place[:, 1].reshape(model_width)
    d_router = everything[:, 2 * model_width + 2 * W :].reshape(expert_total, model_width).T

    return (
        output,
        grad_inputs.reshape(1, row_total, model_width),
        d_attn_gain,
        d_query_gain,
        d_key_gain,
        d_qkv[0],
        d_qkv[1],
        d_qkv[2],
        d_output,
        d_ffn_gain,
        d_router,
        d_experts,
    )


def solution(mesh):
    placed = (
        P("fsdp", "ctx", None),
        P(),
        P(),
        P(),
        P(("ctx", "fsdp"), None),
        P(("ctx", "fsdp"), None),
        P(("ctx", "fsdp"), None),
        P(("ctx", "fsdp"), None),
        P(),
        P(),
        P("ctx", "fsdp", None),
        P("fsdp", "ctx", None),
        P("fsdp", "ctx", None),
    )
    return jax.shard_map(
        layer,
        mesh=mesh,
        in_specs=placed,
        out_specs=(
            P("fsdp", "ctx", None),
            P("fsdp", "ctx", None),
            P(),
            P(),
            P(),
            P(("ctx", "fsdp"), None),
            P(("ctx", "fsdp"), None),
            P(("ctx", "fsdp"), None),
            P(("ctx", "fsdp"), None),
            P(),
            P(),
            P("ctx", "fsdp", None),
        ),
        check_vma=False,
    )
```

profile of v0, /device:TPU:0, one launch (start us, length us, event | category | flops | bytes accessed | tf_op | source)
XLA Modules:
  0.0 917.4 jit_solution(5424119287309756646)
XLA Ops:
  11.2 16.5 %all_to_all.20 = bf16[4,64,1536]{2,1,0:T(8,128)(2,1)S(1)} all-to-all(bf16[4,64,1536]{2,1,0:T(8,128)(2,1)S(1)} %copy.86), channel_id=1, replica_groups=mesh['ctx'=4,'fsdp'=8] {'ctx'}, dimensions={0} | all-to-all | bytes 1572864 | tf_op jit(solution)/shard_map/all_to_all | solution.py:587
  33.6 15.4 %all-gather = s32[1,1024,8]{1,2,0:T(8,128)S(1)} all-gather(s32[1,128,8]{1,2,0:T(8,128)S(1)} %copy-done.104), channel_id=2, replica_groups=mesh['ctx'=4,'fsdp'=8] {'fsdp'}, dimensions={1}, use_global_device_ids=true | all-gather | bytes 36864 | tf_op jit(solution)/shard_map/all_gather | solution.py:582
  57.4 36.5 %all-gather.7.cloned.1.call-done = bf16[4,512,1536]{2,0,1:T(4,128)(2,1)} async-done(((bf16[4,64,1536]{2,0,1:T(4,128)(2,1)}), bf16[4,512,1536]{2,0,1:T(4,128)(2,1)}) %all-gather.7.cloned.1.call-update) | async-done | bytes 6291472 | tf_op jit(solution)/shard_map/all_gather | solution.py:594
  157.0 13.3 %copy.129 = bf16[512,4,3072]{2,0,1:T(8,128)(2,1)} copy(bf16[512,4,3072]{2,1,0:T(4,128)(2,1)} %param.23) | data formatting | bytes 25165824 | tf_op jit(solution)/shard_map/optimization_barrier | solution.py:598
  185.2 31.9 %collective-permute-done.14.refs_7_ = bf16[256,3072]{1,0:T(8,128)(2,1)S(1)} collective-permute-done((bf16[256,3072]{1,0:T(8,128)(2,1)S(1)}, bf16[256,3072]{1,0:T(8,128)(2,1)S(1)}, u32[]{:S(2)}, u32[]{:S(2)}) %collective-permute-start.14) | collective-permute-done | bytes 1572896 | tf_op jit(solution)/shard_map/ppermute | solution.py:57
  220.0 31.0 %collective-permute-done.13.refs_6_ = bf16[256,3072]{1,0:T(8,128)(2,1)} collective-permute-done((bf16[256,3072]{1,0:T(8,128)(2,1)}, bf16[256,3072]{1,0:T(8,128)(2,1)}, u32[]{:S(2)}, u32[]{:S(2)}) %collective-permute-start.13) | collective-permute-done | bytes 1572896 | tf_op jit(solution)/shard_map/ppermute | solution.py:57
  250.9 29.5 %collective-permute-done.12.refs_5_ = bf16[256,3072]{1,0:T(8,128)(2,1)} collective-permute-done((bf16[256,3072]{1,0:T(8,128)(2,1)}, bf16[256,3072]{1,0:T(8,128)(2,1)}, u32[]{:S(2)}, u32[]{:S(2)}) %collective-permute-start.12) | collective-permute-done | bytes 1572896 | tf_op jit(solution)/shard_map/ppermute | solution.py:57
  280.4 33.6 %collective-permute-done.11.refs_4_ = bf16[256,3072]{1,0:T(8,128)(2,1)} collective-permute-done((bf16[256,3072]{1,0:T(8,128)(2,1)}, bf16[256,3072]{1,0:T(8,128)(2,1)}, u32[]{:S(2)}, u32[]{:S(2)}) %collective-permute-start.11) | collective-permute-done | bytes 1572896 | tf_op jit(solution)/shard_map/ppermute | solution.py:57
  352.9 14.3 %expert.4 = (bf16[272,2176]{1,0:T(8,128)(2,1)}, bf16[272,2048]{1,0:T(8,128)(2,1)S(1)}, bf16[272,2048]{1,0:T(8,128)(2,1)S(1)}, bf16[272,1024]{1,0:T(8,128)(2,1)S(...) custom-call(s32[1]{0:T(128)} %bitcast.26.mine_ref, ...), custom_call_target="tpu_custom_call" | custom-call | flops 6845104128 | bytes 18153472 | tf_op jit(solution)/shard_map/expert/pallas_call | solution.py:261
  369.6 13.2 %collective-permute-done.22.cots_ref = bf16[272,2048]{1,0:T(8,128)(2,1)S(1)} collective-permute-done((bf16[272,2048]{1,0:T(8,128)(2,1)}, bf16[272,2048]{1,0:T(8,128)(2,1)S(1)}, u32[]{:S(2)}, u32[]{:S(2)}) %collective-permute-start.22) | collective-permute-done | bytes 1114144 | tf_op jit(solution)/shard_map/ppermute | solution.py:57
  384.6 22.0 %collective-permute-done.21.rows_ref.refs_15_ = bf16[272,2048]{1,0:T(8,128)(2,1)S(1)} collective-permute-done((bf16[272,2048]{1,0:T(8,128)(2,1)}, bf16[272,2048]{1,0:T(8,128)(2,1)S(1)}, u32[]{:S(2)}, u32[]{:S(2)}) %collective-permute-start.21) | collective-permute-done | bytes 1114144 | tf_op jit(solution)/shard_map/ppermute | solution.py:57
  406.6 14.1 %expert.7 = (bf16[272,2176]{1,0:T(8,128)(2,1)}, bf16[272,2048]{1,0:T(8,128)(2,1)S(1)}, bf16[272,2048]{1,0:T(8,128)(2,1)S(1)}, bf16[272,1024]{1,0:T(8,128)(2,1)S(...) custom-call(s32[1]{0:T(128)} %bitcast.26.mine_ref, ...), custom_call_target="tpu_custom_call" | custom-call | flops 6845104128 | bytes 18153472 | tf_op jit(solution)/shard_map/expert/pallas_call | solution.py:261
  426.8 34.5 %collective-permute-done.18.rows_ref.refs_10_ = bf16[272,2048]{1,0:T(8,128)(2,1)S(1)} collective-permute-done((bf16[272,2048]{1,0:T(8,128)(2,1)S(1)}, bf16[272,2048]{1,0:T(8,128)(2,1)S(1)}, u32[]{:S(2)}, u32[]{:S(2)}) %collective-permute-start.18) | collective-permute-done | bytes 1114144 | tf_op jit(solution)/shard_map/ppermute | solution.py:57
  461.3 14.1 %expert.6 = (bf16[272,2176]{1,0:T(8,128)(2,1)}, bf16[272,2048]{1,0:T(8,128)(2,1)S(1)}, bf16[272,2048]{1,0:T(8,128)(2,1)S(1)}, bf16[272,1024]{1,0:T(8,128)(2,1)S(...) custom-call(s32[1]{0:T(128)} %bitcast.26.mine_ref, ...), custom_call_target="tpu_custom_call" | custom-call | flops 6845104128 | bytes 18153472 | tf_op jit(solution)/shard_map/expert/pallas_call | solution.py:261
  481.2 14.1 %expert.5 = (bf16[272,2176]{1,0:T(8,128)(2,1)}, bf16[272,2048]{1,0:T(8,128)(2,1)S(1)}, bf16[272,2048]{1,0:T(8,128)(2,1)S(1)}, bf16[272,1024]{1,0:T(8,128)(2,1)S(...) custom-call(s32[1]{0:T(128)} %bitcast.26.mine_ref, ...), custom_call_target="tpu_custom_call" | custom-call | flops 6845104128 | bytes 18153472 | tf_op jit(solution)/shard_map/expert/pallas_call | solution.py:261
  506.7 19.9 %collective-permute-done.17.refs_5_ = bf16[272,2176]{1,0:T(8,128)(2,1)S(1)} collective-permute-done((bf16[272,2176]{1,0:T(8,128)(2,1)}, bf16[272,2176]{1,0:T(8,128)(2,1)S(1)}, u32[]{:S(2)}, u32[]{:S(2)}) %collective-permute-start.17) | collective-permute-done | bytes 1183776 | tf_op jit(solution)/shard_map/ppermute | solution.py:57
  526.7 12.9 %collect_rows.2 = bf16[1024,2176]{1,0:T(8,128)(2,1)} custom-call(bf16[1024,272]{1,0:T(8,128)(2,1)S(1)} %copy-done.58, bf16[1024,272]{1,0:T(8,128)(2,1)S(1)} %copy-done.57, bf16[1024,272]{1,0:T(8,128)(2,1)S(1)} %copy-done.56, bf16[1024,272]{1,0:T(8,128)(2,1)S(1)} %copy-done.55, bf16[272,2176]{1,0:T(8,128)(2,1)S(1)} %copy-done.62, ...), custom_call_target="tpu_custom_call" | custom-call | flops 4848615424 | bytes 11419648 | tf_op jit(solution)/shard_map/collect_rows/pallas_call | solution.py:373
  543.3 25.1 %collective-permute-done.32.refs_7_ = bf16[272,2048]{1,0:T(8,128)(2,1)S(1)} collective-permute-done((bf16[272,2048]{1,0:T(8,128)(2,1)}, bf16[272,2048]{1,0:T(8,128)(2,1)S(1)}, u32[]{:S(2)}, u32[]{:S(2)}) %collective-permute-start.32) | collective-permute-done | bytes 1114144 | tf_op jit(solution)/shard_map/ppermute | solution.py:57
  568.3 20.6 %collective-permute-done.31.refs_6_ = bf16[272,2048]{1,0:T(8,128)(2,1)S(1)} collective-permute-done((bf16[272,2048]{1,0:T(8,128)(2,1)}, bf16[272,2048]{1,0:T(8,128)(2,1)S(1)}, u32[]{:S(2)}, u32[]{:S(2)}) %collective-permute-start.31) | collective-permute-done | bytes 1114144 | tf_op jit(solution)/shard_map/ppermute | solution.py:57
  592.4 11.6 %collect_rows.3 = bf16[1024,2048]{1,0:T(8,128)(2,1)} custom-call(bf16[1024,272]{1,0:T(8,128)(2,1)S(1)} %copy-done.59, bf16[1024,272]{1,0:T(8,128)(2,1)S(1)} %copy-done.57, bf16[1024,272]{1,0:T(8,128)(2,1)S(1)} %copy-done.56, bf16[1024,272]{1,0:T(8,128)(2,1)S(1)} %copy-done.55, bf16[272,2048]{1,0:T(8,128)(2,1)S(1)} %copy-done.64, ...), custom_call_target="tpu_custom_call" | custom-call | flops 4563402752 | bytes 10878976 | tf_op jit(solution)/shard_map/collect_rows/pallas_call | solution.py:373
  612.7 12.2 %collective-permute-done.26 = bf16[128,2048]{1,0:T(8,128)(2,1)S(1)} collective-permute-done((bf16[128,2048]{1,0:T(8,128)(2,1)S(1)}, bf16[128,2048]{1,0:T(8,128)(2,1)S(1)}, u32[]{:S(2)}, u32[]{:S(2)}) %collective-permute-start.26) | collective-permute-done | bytes 524320 | tf_op jit(solution)/shard_map/ppermute | solution.py:57
  642.8 12.4 %attend_back.1 = (f32[512,512]{1,0:T(8,128)}, f32[512,512]{1,0:T(8,128)}, bf16[512,512]{1,0:T(8,128)(2,1)}, f32[512,2]{1,0:T(8,128)}, f32[2,512]{1,0:T(2,128)}) custom-call(f32[512,1536]{1,0:T(8,128)} %copy-done, f32[512,1536]{1,0:T(8,128)} %copy-done, f32[512,1536]{1,0:T(8,128)} %copy-done, f32[512,2]{1,0:T(8,128)} %bitcast.187, f32[2,512]{1,0:T(2,128)} %copy-done.60, ...), custom_call_target="tpu_custom_call" | custom-call | flops 1610612736 | bytes 6291456 | tf_op jit(solution)/shard_map/attend_back/pallas_call | solution.py:514
  749.3 28.0 %all-to-all-done.1 = f32[32,16,128]{2,1,0:T(8,128)} async-done(((f32[32,16,128]{2,1,0:T(8,128)}), f32[32,16,128]{2,1,0:T(8,128)}, u32[]{:S(2)}, u32[]{:S(2)}) %all-to-all-start.1) | async-done | bytes 262176 | tf_op jit(solution)/shard_map/all_to_all | solution.py:743
  827.4 46.5 %collective-permute-done.40.refs_2_ = bf16[256,3072]{1,0:T(8,128)(2,1)} collective-permute-done((bf16[256,3072]{1,0:T(8,128)(2,1)}, bf16[256,3072]{1,0:T(8,128)(2,1)}, u32[]{:S(2)}, u32[]{:S(2)}) %collective-permute-start.40) | collective-permute-done | bytes 1572896 | tf_op jit(solution)/shard_map/ppermute | solution.py:57
  (443 shorter events, 378.7 us)
Async XLA Ops:
  7.2 86.6 %all-gather.7.cloned.1.call-start = ((), (), s32[]{:S(2)}) async-start(), calls=%async_computation.8 | async-start | bytes 7077888 | tf_op jit(solution)/shard_map/all_gather | solution.py:594
  29.1 95.5 %all-gather.9.cloned.1.call-start = ((), (), s32[]{:S(2)}) async-start(), calls=%async_computation.9 | async-start | bytes 2359296 | tf_op jit(solution)/shard_map/all_gather | solution.py:595
  29.9 296.1 %all-gather.13.cloned.1.call-start = ((), (), s32[]{:S(2)}) async-start(), calls=%async_computation.15 | async-start | bytes 4718592 | tf_op jit(solution)/shard_map/all_gather | solution.py:657
  33.5 308.2 %all-gather.11.cloned.1.call-start = ((), (), s32[]{:S(2)}) async-start(), calls=%async_computation.10 | async-start | bytes 4718592 | tf_op jit(solution)/shard_map/all_gather | solution.py:696
  156.8 448.8 %reduce-scatter.5.cloned.1.call-start = ((), (), s32[]{:S(2)}) async-start(), calls=%async_computation.11 | async-start | bytes 5013504 | tf_op jit(solution)/shard_map/reduce_scatter | solution.py:707
  181.9 98.5 %collective-permute-start.12 = (bf16[256,3072]{1,0:T(8,128)(2,1)}, bf16[256,3072]{1,0:T(8,128)(2,1)}, u32[]{:S(2)}, u32[]{:S(2)}) collective-permute-start(bf16[256,3072]{1,0:T(8,128)(2,1)} %get-tuple-element.145), channel_id=1, source_target_pairs={{0,16},{8,24},{16,0},{24,8},{1,17},{9,25},{17,1},{25,9},{2,18},{10... | collective-permute-start | bytes 4718600 | tf_op jit(solution)/shard_map/ppermute | solution.py:57
  182.4 131.6 %collective-permute-start.11 = (bf16[256,3072]{1,0:T(8,128)(2,1)}, bf16[256,3072]{1,0:T(8,128)(2,1)}, u32[]{:S(2)}, u32[]{:S(2)}) collective-permute-start(bf16[256,3072]{1,0:T(8,128)(2,1)} %get-tuple-element.146), channel_id=1, source_target_pairs={{0,16},{8,24},{16,0},{24,8},{1,17},{9,25},{17,1},{25,9},{2,18},{10... | collective-permute-start | bytes 4718600 | tf_op jit(solution)/shard_map/ppermute | solution.py:57
  183.9 130.1 %collective-permute-start.10 = (bf16[256,3072]{1,0:T(8,128)(2,1)}, bf16[256,3072]{1,0:T(8,128)(2,1)}, u32[]{:S(2)}, u32[]{:S(2)}) collective-permute-start(bf16[256,3072]{1,0:T(8,128)(2,1)} %get-tuple-element.147), channel_id=1, source_target_pairs={{0,8},{8,0},{16,24},{24,16},{1,9},{9,1},{17,25},{25,17},{2,10},{10... | collective-permute-start | bytes 4718600 | tf_op jit(solution)/shard_map/ppermute | solution.py:57
  218.3 95.7 %collective-permute-start.9 = (bf16[256,3072]{1,0:T(8,128)(2,1)}, bf16[256,3072]{1,0:T(8,128)(2,1)}, u32[]{:S(2)}, u32[]{:S(2)}) collective-permute-start(bf16[256,3072]{1,0:T(8,128)(2,1)} %get-tuple-element.148), channel_id=1, source_target_pairs={{0,8},{8,0},{16,24},{24,16},{1,9},{9,1},{17,25},{25,17},{2,10},{10... | collective-permute-start | bytes 4718600 | tf_op jit(solution)/shard_map/ppermute | solution.py:57
  330.7 150.5 %collective-permute-start.16 = (bf16[272,2048]{1,0:T(8,128)(2,1)}, bf16[272,2048]{1,0:T(8,128)(2,1)}, u32[]{:S(2)}, u32[]{:S(2)}) collective-permute-start(bf16[272,2048]{1,0:T(8,128)(2,1)} %fusion.14), channel_id=1, source_target_pairs={{0,8},{8,0},{16,24},{24,16},{1,9},{9,1},{17,25},{25,17},{2,10},{10... | collective-permute-start | bytes 3342344 | tf_op jit(solution)/shard_map/ppermute | solution.py:57
  338.1 88.7 %collective-permute-start.19 = (bf16[272,2048]{1,0:T(8,128)(2,1)}, bf16[272,2048]{1,0:T(8,128)(2,1)S(1)}, u32[]{:S(2)}, u32[]{:S(2)}) collective-permute-start(bf16[272,2048]{1,0:T(8,128)(2,1)} %fusion.17), channel_id=1, source_target_pairs={{0,16},{8,24},{16,0},{24,8},{1,17},{9,25},{17,1},{25,9},{2,18},{10... | collective-permute-start | bytes 3342344 | tf_op jit(solution)/shard_map/ppermute | solution.py:57
  345.6 115.7 %collective-permute-start.18 = (bf16[272,2048]{1,0:T(8,128)(2,1)S(1)}, bf16[272,2048]{1,0:T(8,128)(2,1)S(1)}, u32[]{:S(2)}, u32[]{:S(2)}) collective-permute-start(bf16[272,2048]{1,0:T(8,128)(2,1)S(1)} %convolution_convert_fusion.3), channel_id=1, source_target_pairs={{0,16},{8,24},{16,0},{24,8},{1,17},{9,25},{17,1},{25,9},{2,18},{10... | collective-permute-start | bytes 3342344 | tf_op jit(solution)/shard_map/ppermute | solution.py:57
  382.8 98.5 %collective-permute-start.15 = (bf16[272,2048]{1,0:T(8,128)(2,1)}, bf16[272,2048]{1,0:T(8,128)(2,1)S(1)}, u32[]{:S(2)}, u32[]{:S(2)}) collective-permute-start(bf16[272,2048]{1,0:T(8,128)(2,1)} %convolution_convert_fusion.4), channel_id=1, source_target_pairs={{0,8},{8,0},{16,24},{24,16},{1,9},{9,1},{17,25},{25,17},{2,10},{10... | collective-permute-start | bytes 3342344 | tf_op jit(solution)/shard_map/ppermute | solution.py:57
  424.1 77.5 %collective-permute-start.23 = (bf16[272,2176]{1,0:T(8,128)(2,1)}, bf16[272,2176]{1,0:T(8,128)(2,1)S(1)}, u32[]{:S(2)}, u32[]{:S(2)}) collective-permute-start(bf16[272,2176]{1,0:T(8,128)(2,1)} %get-tuple-element.87), channel_id=1, source_target_pairs={{0,24},{8,16},{16,8},{24,0},{1,25},{9,17},{17,9},{25,1},{2,26},{10... | collective-permute-start | bytes 3551240 | tf_op jit(solution)/shard_map/ppermute | solution.py:57
  539.6 352.3 %reduce-scatter.7.cloned.1.call-start = ((), (), s32[]{:S(2)}) async-start(), calls=%async_computation.12 | async-start | bytes 4718592 | tf_op jit(solution)/shard_map/reduce_scatter | solution.py:729
  604.0 290.0 %reduce-scatter.9.cloned.1.call-start = ((), (), s32[]{:S(2)}) async-start(), calls=%async_computation.13 | async-start | bytes 7077888 | tf_op jit(solution)/shard_map/reduce_scatter | solution.py:771
  702.5 182.6 %collective-permute-start.38 = (bf16[256,3072]{1,0:T(8,128)(2,1)}, bf16[256,3072]{1,0:T(8,128)(2,1)}, u32[]{:S(2)}, u32[]{:S(2)}) collective-permute-start(bf16[256,3072]{1,0:T(8,128)(2,1)} %get-tuple-element.119), channel_id=1, source_target_pairs={{0,24},{8,16},{16,8},{24,0},{1,25},{9,17},{17,9},{25,1},{2,26},{10... | collective-permute-start | bytes 4718600 | tf_op jit(solution)/shard_map/ppermute | solution.py:57
  703.8 100.2 %collective-permute-start.41 = (bf16[256,3072]{1,0:T(8,128)(2,1)}, bf16[256,3072]{1,0:T(8,128)(2,1)}, u32[]{:S(2)}, u32[]{:S(2)}) collective-permute-start(bf16[256,3072]{1,0:T(8,128)(2,1)} %get-tuple-element.123), channel_id=1, source_target_pairs={{0,24},{8,16},{16,8},{24,0},{1,25},{9,17},{17,9},{25,1},{2,26},{10... | collective-permute-start | bytes 4718600 | tf_op jit(solution)/shard_map/ppermute | solution.py:57
  723.6 179.2 %reduce-scatter.11.cloned.1.call-start = ((), (), s32[]{:S(2)}) async-start(), calls=%async_computation.14 | async-start | bytes 2359296 | tf_op jit(solution)/shard_map/reduce_scatter | solution.py:750
  788.8 96.4 %collective-permute-start.37 = (bf16[256,3072]{1,0:T(8,128)(2,1)}, bf16[256,3072]{1,0:T(8,128)(2,1)}, u32[]{:S(2)}, u32[]{:S(2)}) collective-permute-start(bf16[256,3072]{1,0:T(8,128)(2,1)} %get-tuple-element.118), channel_id=1, source_target_pairs={{0,16},{8,24},{16,0},{24,8},{1,17},{9,25},{17,1},{25,9},{2,18},{10... | collective-permute-start | bytes 4718600 | tf_op jit(solution)/shard_map/ppermute | solution.py:57
  798.8 75.0 %collective-permute-start.40 = (bf16[256,3072]{1,0:T(8,128)(2,1)}, bf16[256,3072]{1,0:T(8,128)(2,1)}, u32[]{:S(2)}, u32[]{:S(2)}) collective-permute-start(bf16[256,3072]{1,0:T(8,128)(2,1)} %get-tuple-element.122), channel_id=1, source_target_pairs={{0,16},{8,24},{16,0},{24,8},{1,17},{9,25},{17,1},{25,9},{2,18},{10... | collective-permute-start | bytes 4718600 | tf_op jit(solution)/shard_map/ppermute | solution.py:57
  800.0 85.2 %collective-permute-start.36 = (bf16[256,3072]{1,0:T(8,128)(2,1)}, bf16[256,3072]{1,0:T(8,128)(2,1)}, u32[]{:S(2)}, u32[]{:S(2)}) collective-permute-start(bf16[256,3072]{1,0:T(8,128)(2,1)} %get-tuple-element.117), channel_id=1, source_target_pairs={{0,8},{8,0},{16,24},{24,16},{1,9},{9,1},{17,25},{25,17},{2,10},{10... | collective-permute-start | bytes 4718600 | tf_op jit(solution)/shard_map/ppermute | solution.py:57
  804.0 73.1 %collective-permute-start.39 = (bf16[256,3072]{1,0:T(8,128)(2,1)}, bf16[256,3072]{1,0:T(8,128)(2,1)}, u32[]{:S(2)}, u32[]{:S(2)}) collective-permute-start(bf16[256,3072]{1,0:T(8,128)(2,1)} %get-tuple-element.121), channel_id=1, source_target_pairs={{0,8},{8,0},{16,24},{24,16},{1,9},{9,1},{17,25},{25,17},{2,10},{10... | collective-permute-start | bytes 4718600 | tf_op jit(solution)/shard_map/ppermute | solution.py:57
  806.4 87.6 %all-to-all-start.2 = ((f32[32,56,128]{2,1,0:T(8,128)}), f32[32,56,128]{2,1,0:T(8,128)}, u32[]{:S(2)}, u32[]{:S(2)}) async-start(f32[32,56,128]{2,1,0:T(8,128)} %broadcast_in_dim.18), calls=%async_computation.4 | async-start | bytes 1835008 | tf_op jit(solution)/shard_map/all_to_all | solution.py:796
  (144 other events, 2588.8 us)
Sparse Core Ops, SparseCore 0:
  29.2 64.5 all-gather.6
  95.4 27.7 all-gather.8
  124.8 46.2 all-gather.12
  173.2 45.6 all-gather.10
  539.8 53.0 reduce-scatter.4
  604.1 50.0 reduce-scatter.6
  684.1 73.8 reduce-scatter.8
  760.3 35.3 reduce-scatter.10
where the time goes:
time: 922 us; the launch traced here: 917 us
  waiting for transfers between devices  460 us (50%)
  Pallas kernels  167 us (18%)
  local copies, waits for them, and re-layouts  90.9 us (10%)
  starting transfers between devices  68.1 us (7%)
  matrix products  53.6 us (6%)
  blocking collectives  31.8 us (3%)
  other arithmetic  30.1 us (3%)
  between operations  15.7 us (2%)
    ppermute x42, waiting for transfers between devices, from_peer(): return lax.ppermute(values, 'ctx', [(i, i ^ offset) for i in range(total)])  393 us
    pallas_call x4, Pallas kernels, run_expert(): pl.pallas_call(functools.partial(expert_kernel, steps), grid_spec=pltpu.P...  56.5 us
    ppermute x42, starting transfers between devices, from_peer(): return lax.ppermute(values, 'ctx', [(i, i ^ offset) for i in range(total)])  54.4 us
    pallas_call x4, Pallas kernels, weight_grad(): pl.pallas_call(functools.partial(weight_kernel, len(groups), steps), grid...  45.4 us
    unnamed x240, local copies, waits for them, and re-layouts  44.4 us
    all_gather x1, waiting for transfers between devices, layer(): lax.all_gather(w_cols, 'fsdp', axis=1, tiled=True)  36.5 us
    dot_general x11, matrix products, mm(): return jnp.dot(a, b, preferred_element_type=f32)  31.3 us
    all_to_all x1, waiting for transfers between devices, layer(): lax.all_to_all(grad_router.reshape(devices, -1, 128), everyone, 0, 0, til...  28 us
  transfers between devices with their start and end apart: 53, of which 25 were waited for; matrix products, arithmetic and copies ran while one was open for 13% of the time, Pallas kernels for 17%

commit v1 on v0

--- a/solution.py
+++ b/solution.py
@@ -171,15 +171,32 @@
     return result
 
 
-def sum_rows(values, total):
-    count, width = values.shape
-    bits = total.bit_length() - 1
-    result = values
+def spread_rows(values, total):
+    return [values] + [from_peer(values, j, total) for j in range(1, total)]
+
+
+def add_rows(refs):
+    total = len(refs)
+    result = refs[0][...]
+    rows = result.shape[1] // total
     for j in range(1, total):
-        other = from_peer(values, j, total).reshape((count,) + (2,) * bits + (width // total,))
-        other = jnp.flip(other, [1 + n for n in range(bits) if j >> (bits - 1 - n) & 1])
-        result = result + other.reshape(count, width)
+        other = refs[j][...]
+        blocks = [other[:, (i ^ j) * rows : ((i ^ j) + 1) * rows] for i in range(total)]
+        result = result + jnp.concatenate(blocks, 1)
     return result
+
+
+def diagonal(size):
+    first = lax.broadcasted_iota(jnp.int32, (size, size), 0)
+    return first == lax.broadcasted_iota(jnp.int32, (size, size), 1)
+
+
+def as_column(row):
+    return jnp.sum(jnp.where(diagonal(row.shape[1]), row, 0.0), 1, keepdims=True)
+
+
+def as_row(column):
+    return jnp.sum(jnp.where(diagonal(column.shape[0]), column, 0.0), 0, keepdims=True)
 
 
 def dot_nn(a, b):
@@ -400,7 +417,15 @@
     return query, key, weights / jnp.sum(weights, -1, keepdims=True)
 
 
-def attend_kernel(q_ref, k_ref, v_ref, scale_ref, gain_ref, cos_ref, sin_ref, rp, cp, out_ref):
+def attend_kernel(model_width, q_ref, k_ref, v_ref, gain_ref, cos_ref, sin_ref, rp, cp, *refs):
+    parts, out_ref, scale_ref = refs[:-2], refs[-2], refs[-1]
+
+    @pl.when(pl.program_id(0) == 0)
+    def _():
+        scale = lax.rsqrt(add_rows(parts) / model_width + epsilon)
+        for n in range(2):
+            scale_ref[:, n : n + 1] = as_column(scale[n : n + 1, :])
+
     _, _, probs = head_forward(
         q_ref[...],
         k_ref[...],
@@ -418,19 +443,21 @@
     q_ref,
     k_ref,
     v_ref,
-    scale_ref,
     gain_ref,
     cos_ref,
     sin_ref,
     rp,
     cp,
+    scale_ref,
     grad_ref,
     yq_ref,
     yk_ref,
     gv_ref,
     dots_ref,
     gains_ref,
+    held,
 ):
+    head = pl.program_id(0)
     raw_q = q_ref[...]
     raw_k = k_ref[...]
     scale = scale_ref[...]
@@ -456,12 +483,75 @@
     dot_q = jnp.sum(part_q * gains[0:1, :], -1, keepdims=True)
     dot_k = jnp.sum(part_k * gains[1:2, :], -1, keepdims=True)
 
-    @pl.when(pl.program_id(0) == 0)
-    def _():
-        dots_ref[...] = jnp.zeros_like(dots_ref)
-
-    column = lax.broadcasted_iota(jnp.int32, dots_ref.shape, 1)
-    dots_ref[...] += jnp.where(column == 0, dot_q, dot_k)
+    @pl.when(head == 0)
+    def _():
+        held[...] = jnp.zeros_like(held)
+
+    held[:, 0:1] += dot_q
+    held[:, 1:2] += dot_k
+
+    @pl.when(head == pl.num_programs(0) - 1)
+    def _():
+        for n in range(2):
+            dots_ref[n : n + 1, :] = as_row(held[:, n : n + 1])
+
+
+def finish_kernel(model_width, heads, yq_ref, yk_ref, gv_ref, raw_ref, gain_ref, scale_ref, *refs):
+    parts, out_ref, dots = refs[:-2], refs[-2], refs[-1]
+    step = pl.program_id(0)
+
+    @pl.when(step == 0)
+    def _():
+        total = add_rows(parts) / model_width
+        for n in range(2):
+            dots[:, n : n + 1] = as_column(total[n : n + 1, :])
+
+    def through(n, grad):
+        scale = scale_ref[:, n : n + 1]
+        cube = scale * scale * scale * dots[:, n : n + 1]
+        out_ref[...] = (scale * (grad * gain_ref[n : n + 1, :]) - raw_ref[...] * cube).astype(bf16)
+
+    @pl.when(step < heads)
+    def _():
+        through(0, yq_ref[...])
+
+    @pl.when((step >= heads) & (step < 2 * heads))
+    def _():
+        through(1, yk_ref[...])
+
+    @pl.when(step >= 2 * heads)
+    def _():
+        out_ref[...] = gv_ref[...]
+
+
+def finish(model_width, yq, yk, gv, raw_qkv, gains, scales, parts):
+    seq, width = gv.shape
+    heads = width // HD
+
+    def block(first, last):
+        return pl.BlockSpec((seq, HD), lambda i: (0, jnp.clip(i - first, 0, last)))
+
+    return pl.pallas_call(
+        functools.partial(finish_kernel, model_width, heads),
+        grid=(3 * heads,),
+        in_specs=[
+            block(0, heads - 1),
+            block(heads, heads - 1),
+            block(2 * heads, heads - 1),
+            block(0, 2 * heads - 1),
+            pl.BlockSpec((2, HD), lambda i: (0, lax.rem(i, heads))),
+            pl.BlockSpec((seq, 2), lambda i: (0, 0)),
+        ]
+        + [pl.BlockSpec((2, seq), lambda i: (0, 0))] * len(parts),
+        out_specs=pl.BlockSpec((seq, HD), lambda i: (0, i)),
+        out_shape=jax.ShapeDtypeStruct((seq, 3 * width), bf16),
+        scratch_shapes=[pltpu.VMEM((seq, 2), f32)],
+        compiler_params=pltpu.CompilerParams(vmem_limit_bytes=48 << 20),
+        cost_estimate=pl.CostEstimate(
+            flops=16 * seq * width, bytes_accessed=26 * seq * width, transcendentals=0
+        ),
+        name="finish",
+    )(yq, yk, gv, raw_qkv, gains, scales, *parts)
 
 
 def head_specs(seq, heads):
@@ -476,27 +566,29 @@
         one,
         key,
         value,
-        fixed((seq, 2)),
         pl.BlockSpec((2, HD), lambda h: (0, h)),
         fixed((seq, HD)),
         fixed((seq, HD)),
         fixed((seq, 1)),
         fixed((1, seq)),
     ]
-    return one, specs
-
-
-def attend(raw_qkv, tables):
+    return one, specs, fixed
+
+
+def attend(raw_qkv, tables, parts, model_width):
     seq = raw_qkv.shape[0]
     width = raw_qkv.shape[1] // 3
     heads = width // HD
-    one, specs = head_specs(seq, heads)
+    one, specs, fixed = head_specs(seq, heads)
     return pl.pallas_call(
-        attend_kernel,
+        functools.partial(attend_kernel, model_width),
         grid=(heads,),
-        in_specs=specs,
-        out_specs=one,
-        out_shape=jax.ShapeDtypeStruct((seq, width), bf16),
+        in_specs=specs + [fixed((2, seq))] * len(parts),
+        out_specs=[one, fixed((seq, 2))],
+        out_shape=[
+            jax.ShapeDtypeStruct((seq, width), bf16),
+            jax.ShapeDtypeStruct((seq, 2), f32),
+        ],
         compiler_params=pltpu.CompilerParams(vmem_limit_bytes=48 << 20),
         cost_estimate=pl.CostEstimate(
             flops=4 * seq * seq * width,
@@ -504,31 +596,26 @@
             transcendentals=seq * seq * heads,
         ),
         name="attend",
-    )(raw_qkv, raw_qkv, raw_qkv, *tables)
-
-
-def attend_back(raw_qkv, tables, grad):
+    )(raw_qkv, raw_qkv, raw_qkv, *tables, *parts)
+
+
+def attend_back(raw_qkv, tables, scales, grad):
     seq, width = grad.shape
     heads = width // HD
-    one, specs = head_specs(seq, heads)
+    one, specs, fixed = head_specs(seq, heads)
     return pl.pallas_call(
         attend_back_kernel,
         grid=(heads,),
-        in_specs=specs + [one],
-        out_specs=[
-            one,
-            one,
-            one,
-            pl.BlockSpec((seq, 2), lambda h: (0, 0)),
-            pl.BlockSpec((2, HD), lambda h: (0, h)),
-        ],
+        in_specs=specs + [fixed((seq, 2)), one],
+        out_specs=[one, one, one, fixed((2, seq)), pl.BlockSpec((2, HD), lambda h: (0, h))],
         out_shape=[
             jax.ShapeDtypeStruct((seq, width), f32),
             jax.ShapeDtypeStruct((seq, width), f32),
             jax.ShapeDtypeStruct((seq, width), bf16),
-            jax.ShapeDtypeStruct((seq, 2), f32),
+            jax.ShapeDtypeStruct((2, seq), f32),
             jax.ShapeDtypeStruct((2, width), f32),
         ],
+        scratch_shapes=[pltpu.VMEM((seq, 2), f32)],
         compiler_params=pltpu.CompilerParams(vmem_limit_bytes=56 << 20),
         cost_estimate=pl.CostEstimate(
             flops=12 * seq * seq * width,
@@ -536,7 +623,7 @@
             transcendentals=seq * seq * heads,
         ),
         name="attend_back",
-    )(raw_qkv, raw_qkv, raw_qkv, *tables, grad)
+    )(raw_qkv, raw_qkv, raw_qkv, *tables, scales, grad)
 
 
 def layer(
@@ -675,18 +762,10 @@
     raw_qkv = mm(normed, w_qkv)
     raw_q = raw_qkv[:, :W]
     raw_k = raw_qkv[:, W : 2 * W]
-    squares = sum_rows(jnp.stack([jnp.sum(raw_q * raw_q, -1), jnp.sum(raw_k * raw_k, -1)]), C)
-    scales = lax.rsqrt(squares / model_width + epsilon).T
+    squares = spread_rows(jnp.stack([jnp.sum(raw_q * raw_q, -1), jnp.sum(raw_k * raw_k, -1)]), C)
     signed_sine = jnp.where(jnp.arange(HD) < HD // 2, -1.0, 1.0) * sine
-    tables = (
-        scales,
-        gains,
-        cosine,
-        signed_sine,
-        positions.reshape(seq, 1),
-        positions.reshape(1, seq),
-    )
-    attended = attend(raw_qkv, tables)
+    tables = (gains, cosine, signed_sine, positions.reshape(seq, 1), positions.reshape(1, seq))
+    attended, scales = attend(raw_qkv, tables, squares, model_width)
     inputs = tokens_low.astype(f32)
     hidden_one = inputs + scatter_rows(mm(attended, w_o), C)
 
@@ -751,23 +830,14 @@
         d_output, "fsdp", scatter_dimension=0, tiled=True
     ).astype(f32)
     grad_q_n, grad_k_n, grad_value, dots, gain_grads = attend_back(
-        raw_qkv, tables, grad_att
-    )
-    dots = sum_rows(dots.T, C)
-    dots = dots / model_width
-    late_hidden, _ = lax.optimization_barrier((hidden_one, dots))
+        raw_qkv, tables, scales, grad_att
+    )
+    dots = spread_rows(dots, C)
+    late_hidden, dots = lax.optimization_barrier((hidden_one, dots))
     output = (late_hidden + mixed).astype(bf16).reshape(1, row_total, model_width)
-    scale_q = scales[:, 0:1]
-    scale_k = scales[:, 1:2]
-    grad_q = (
-        scale_q * grad_q_n * gains[0]
-        - raw_qkv[:, :W] * scale_q * scale_q * scale_q * dots[0][:, None]
-    ).astype(bf16)
-    grad_k = (
-        scale_k * grad_k_n * gains[1]
-        - raw_qkv[:, W : 2 * W] * scale_k * scale_k * scale_k * dots[1][:, None]
-    ).astype(bf16)
-    grad_qkv = jnp.concatenate([grad_q, grad_k, grad_value], 1)
+    grad_qkv = finish(
+        model_width, grad_q_n, grad_k_n, grad_value, raw_qkv, gains, scales, dots
+    )
     d_cols = lax.psum_scatter(
         mm_tn(normed, grad_qkv).astype(bf16).reshape(C, F * shard, 3 * W),
         "fsdp",

time: 922 us -> 913 us (level)
    pallas_call x2 -> x3, Pallas kernels: 18.6 us -> 25.4 us  [the longest x1 12.7 us: attend_back(): pl.pallas_call(attend_back_kernel, grid=(heads,), in_specs=specs + [fixed...]
    unnamed x240 -> x268, local copies, waits for them, and re-layouts: 44.4 us -> 45.8 us
  transfers between devices with their start and end apart: 53 -> 53, of which waited for: 25 -> 30; matrix products, arithmetic and copies ran while one was open for 13% -> 12% of each run, Pallas kernels for 17% -> 18%
where the time goes in v1:
time: 913 us; the launch traced here: 909 us
  waiting for transfers between devices  460 us (50%)
  Pallas kernels  174 us (19%)
  local copies, waits for them, and re-layouts  83.3 us (9%)
  starting transfers between devices  64.8 us (7%)
  matrix products  54.6 us (6%)
  blocking collectives  31.6 us (3%)
  other arithmetic  24.5 us (3%)
  between operations  15.6 us (2%)
    ppermute x42, waiting for transfers between devices, from_peer(): return lax.ppermute(values, 'ctx', [(i, i ^ offset) for i in range(total)])  387 us
    pallas_call x4, Pallas kernels, run_expert(): pl.pallas_call(functools.partial(expert_kernel, steps), grid_spec=pltpu.P...  56.5 us
    ppermute x42, starting transfers between devices, from_peer(): return lax.ppermute(values, 'ctx', [(i, i ^ offset) for i in range(total)])  53.4 us
    unnamed x268, local copies, waits for them, and re-layouts  45.8 us
    pallas_call x4, Pallas kernels, weight_grad(): pl.pallas_call(functools.partial(weight_kernel, len(groups), steps), grid...  45.4 us
    all_gather x1, waiting for transfers between devices, layer(): lax.all_gather(w_cols, 'fsdp', axis=1, tiled=True)  36.7 us
    dot_general x11, matrix products, mm(): return jnp.dot(a, b, preferred_element_type=f32)  32.2 us
    all_to_all x1, waiting for transfers between devices, layer(): lax.all_to_all(grad_router.reshape(devices, -1, 128), everyone, 0, 0, til...  29.3 us
  transfers between devices with their start and end apart: 53, of which 30 were waited for; matrix products, arithmetic and copies ran while one was open for 12% of the time, Pallas kernels for 18%

profile of v1, /device:TPU:0, one launch (start us, length us, event | category | flops | bytes accessed | tf_op | source)
XLA Modules:
  0.0 908.5 jit_solution(8307969683325326231)
XLA Ops:
  11.2 16.5 %all_to_all.20 = bf16[4,64,1536]{2,1,0:T(8,128)(2,1)S(1)} all-to-all(bf16[4,64,1536]{2,1,0:T(8,128)(2,1)S(1)} %copy.78), channel_id=1, replica_groups=mesh['ctx'=4,'fsdp'=8] {'ctx'}, dimensions={0} | all-to-all | bytes 1572864 | tf_op jit(solution)/shard_map/all_to_all | solution.py:674
  34.2 15.1 %all-gather = s32[1,1024,8]{1,2,0:T(8,128)S(1)} all-gather(s32[1,128,8]{1,2,0:T(8,128)S(1)} %copy-done.113), channel_id=2, replica_groups=mesh['ctx'=4,'fsdp'=8] {'fsdp'}, dimensions={1}, use_global_device_ids=true | all-gather | bytes 36864 | tf_op jit(solution)/shard_map/all_gather | solution.py:669
  57.1 36.7 %all-gather.7.cloned.1.call-done = bf16[4,512,1536]{2,0,1:T(4,128)(2,1)} async-done(((bf16[4,64,1536]{2,0,1:T(4,128)(2,1)}), bf16[4,512,1536]{2,0,1:T(4,128)(2,1)}) %all-gather.7.cloned.1.call-update) | async-done | bytes 6291472 | tf_op jit(solution)/shard_map/all_gather | solution.py:681
  156.9 13.3 %copy.114 = bf16[512,4,3072]{2,0,1:T(8,128)(2,1)} copy(bf16[512,4,3072]{2,1,0:T(4,128)(2,1)} %param.23) | data formatting | bytes 25165824 | tf_op jit(solution)/shard_map/optimization_barrier | solution.py:685
  184.6 31.9 %collective-permute-done.14.refs_7_ = bf16[256,3072]{1,0:T(8,128)(2,1)S(1)} collective-permute-done((bf16[256,3072]{1,0:T(8,128)(2,1)S(1)}, bf16[256,3072]{1,0:T(8,128)(2,1)S(1)}, u32[]{:S(2)}, u32[]{:S(2)}) %collective-permute-start.14) | collective-permute-done | bytes 1572896 | tf_op jit(solution)/shard_map/ppermute | solution.py:57
  220.1 30.2 %collective-permute-done.13.refs_6_ = bf16[256,3072]{1,0:T(8,128)(2,1)} collective-permute-done((bf16[256,3072]{1,0:T(8,128)(2,1)}, bf16[256,3072]{1,0:T(8,128)(2,1)}, u32[]{:S(2)}, u32[]{:S(2)}) %collective-permute-start.13) | collective-permute-done | bytes 1572896 | tf_op jit(solution)/shard_map/ppermute | solution.py:57
  250.2 31.7 %collective-permute-done.12.refs_5_ = bf16[256,3072]{1,0:T(8,128)(2,1)} collective-permute-done((bf16[256,3072]{1,0:T(8,128)(2,1)}, bf16[256,3072]{1,0:T(8,128)(2,1)}, u32[]{:S(2)}, u32[]{:S(2)}) %collective-permute-start.12) | collective-permute-done | bytes 1572896 | tf_op jit(solution)/shard_map/ppermute | solution.py:57
  281.9 33.6 %collective-permute-done.11.refs_4_ = bf16[256,3072]{1,0:T(8,128)(2,1)} collective-permute-done((bf16[256,3072]{1,0:T(8,128)(2,1)}, bf16[256,3072]{1,0:T(8,128)(2,1)}, u32[]{:S(2)}, u32[]{:S(2)}) %collective-permute-start.11) | collective-permute-done | bytes 1572896 | tf_op jit(solution)/shard_map/ppermute | solution.py:57
  353.1 14.2 %expert.4 = (bf16[272,2176]{1,0:T(8,128)(2,1)}, bf16[272,2048]{1,0:T(8,128)(2,1)S(1)}, bf16[272,2048]{1,0:T(8,128)(2,1)S(1)}, bf16[272,1024]{1,0:T(8,128)(2,1)S(...) custom-call(s32[1]{0:T(128)} %bitcast.19.mine_ref, ...), custom_call_target="tpu_custom_call" | custom-call | flops 6845104128 | bytes 18153472 | tf_op jit(solution)/shard_map/expert/pallas_call | solution.py:278
  369.8 12.8 %collective-permute-done.22.cots_ref = bf16[272,2048]{1,0:T(8,128)(2,1)S(1)} collective-permute-done((bf16[272,2048]{1,0:T(8,128)(2,1)}, bf16[272,2048]{1,0:T(8,128)(2,1)S(1)}, u32[]{:S(2)}, u32[]{:S(2)}) %collective-permute-start.22) | collective-permute-done | bytes 1114144 | tf_op jit(solution)/shard_map/ppermute | solution.py:57
  384.0 22.4 %collective-permute-done.21.rows_ref.refs_15_ = bf16[272,2048]{1,0:T(8,128)(2,1)S(1)} collective-permute-done((bf16[272,2048]{1,0:T(8,128)(2,1)}, bf16[272,2048]{1,0:T(8,128)(2,1)S(1)}, u32[]{:S(2)}, u32[]{:S(2)}) %collective-permute-start.21) | collective-permute-done | bytes 1114144 | tf_op jit(solution)/shard_map/ppermute | solution.py:57
  406.4 14.1 %expert.7 = (bf16[272,2176]{1,0:T(8,128)(2,1)}, bf16[272,2048]{1,0:T(8,128)(2,1)S(1)}, bf16[272,2048]{1,0:T(8,128)(2,1)S(1)}, bf16[272,1024]{1,0:T(8,128)(2,1)S(...) custom-call(s32[1]{0:T(128)} %bitcast.19.mine_ref, ...), custom_call_target="tpu_custom_call" | custom-call | flops 6845104128 | bytes 18153472 | tf_op jit(solution)/shard_map/expert/pallas_call | solution.py:278
  426.3 34.6 %collective-permute-done.18.rows_ref.refs_10_ = bf16[272,2048]{1,0:T(8,128)(2,1)S(1)} collective-permute-done((bf16[272,2048]{1,0:T(8,128)(2,1)}, bf16[272,2048]{1,0:T(8,128)(2,1)S(1)}, u32[]{:S(2)}, u32[]{:S(2)}) %collective-permute-start.18) | collective-permute-done | bytes 1114144 | tf_op jit(solution)/shard_map/ppermute | solution.py:57
  460.9 14.1 %expert.6 = (bf16[272,2176]{1,0:T(8,128)(2,1)}, bf16[272,2048]{1,0:T(8,128)(2,1)S(1)}, bf16[272,2048]{1,0:T(8,128)(2,1)S(1)}, bf16[272,1024]{1,0:T(8,128)(2,1)S(...) custom-call(s32[1]{0:T(128)} %bitcast.19.mine_ref, ...), custom_call_target="tpu_custom_call" | custom-call | flops 6845104128 | bytes 18153472 | tf_op jit(solution)/shard_map/expert/pallas_call | solution.py:278
  481.0 14.2 %expert.5 = (bf16[272,2176]{1,0:T(8,128)(2,1)}, bf16[272,2048]{1,0:T(8,128)(2,1)S(1)}, bf16[272,2048]{1,0:T(8,128)(2,1)S(1)}, bf16[272,1024]{1,0:T(8,128)(2,1)S(...) custom-call(s32[1]{0:T(128)} %bitcast.19.mine_ref, ...), custom_call_target="tpu_custom_call" | custom-call | flops 6845104128 | bytes 18153472 | tf_op jit(solution)/shard_map/expert/pallas_call | solution.py:278
  506.2 19.9 %collective-permute-done.17.refs_5_ = bf16[272,2176]{1,0:T(8,128)(2,1)S(1)} collective-permute-done((bf16[272,2176]{1,0:T(8,128)(2,1)}, bf16[272,2176]{1,0:T(8,128)(2,1)S(1)}, u32[]{:S(2)}, u32[]{:S(2)}) %collective-permute-start.17) | collective-permute-done | bytes 1183776 | tf_op jit(solution)/shard_map/ppermute | solution.py:57
  526.2 12.8 %collect_rows.2 = bf16[1024,2176]{1,0:T(8,128)(2,1)} custom-call(bf16[1024,272]{1,0:T(8,128)(2,1)S(1)} %copy-done.60, bf16[1024,272]{1,0:T(8,128)(2,1)S(1)} %copy-done.59, bf16[1024,272]{1,0:T(8,128)(2,1)S(1)} %copy-done.58, bf16[1024,272]{1,0:T(8,128)(2,1)S(1)} %copy-done.57, bf16[272,2176]{1,0:T(8,128)(2,1)S(1)} %copy-done.66, ...), custom_call_target="tpu_custom_call" | custom-call | flops 4848615424 | bytes 11419648 | tf_op jit(solution)/shard_map/collect_rows/pallas_call | solution.py:390
  542.6 25.1 %collective-permute-done.32.refs_7_ = bf16[272,2048]{1,0:T(8,128)(2,1)S(1)} collective-permute-done((bf16[272,2048]{1,0:T(8,128)(2,1)}, bf16[272,2048]{1,0:T(8,128)(2,1)S(1)}, u32[]{:S(2)}, u32[]{:S(2)}) %collective-permute-start.32) | collective-permute-done | bytes 1114144 | tf_op jit(solution)/shard_map/ppermute | solution.py:57
  567.7 20.4 %collective-permute-done.31.refs_6_ = bf16[272,2048]{1,0:T(8,128)(2,1)S(1)} collective-permute-done((bf16[272,2048]{1,0:T(8,128)(2,1)}, bf16[272,2048]{1,0:T(8,128)(2,1)S(1)}, u32[]{:S(2)}, u32[]{:S(2)}) %collective-permute-start.31) | collective-permute-done | bytes 1114144 | tf_op jit(solution)/shard_map/ppermute | solution.py:57
  590.3 11.6 %collect_rows.3 = bf16[1024,2048]{1,0:T(8,128)(2,1)} custom-call(bf16[1024,272]{1,0:T(8,128)(2,1)S(1)} %copy-done.60, bf16[1024,272]{1,0:T(8,128)(2,1)S(1)} %copy-done.59, bf16[1024,272]{1,0:T(8,128)(2,1)S(1)} %copy-done.58, bf16[1024,272]{1,0:T(8,128)(2,1)S(1)} %copy-done.57, bf16[272,2048]{1,0:T(8,128)(2,1)S(1)} %copy-done.68, ...), custom_call_target="tpu_custom_call" | custom-call | flops 4563402752 | bytes 10878976 | tf_op jit(solution)/shard_map/collect_rows/pallas_call | solution.py:390
  610.5 12.3 %collective-permute-done.26 = bf16[128,2048]{1,0:T(8,128)(2,1)S(1)} collective-permute-done((bf16[128,2048]{1,0:T(8,128)(2,1)S(1)}, bf16[128,2048]{1,0:T(8,128)(2,1)S(1)}, u32[]{:S(2)}, u32[]{:S(2)}) %collective-permute-start.26) | collective-permute-done | bytes 524320 | tf_op jit(solution)/shard_map/ppermute | solution.py:57
  640.6 12.7 %attend_back.1 = (f32[512,512]{1,0:T(8,128)}, f32[512,512]{1,0:T(8,128)}, bf16[512,512]{1,0:T(8,128)(2,1)}, f32[2,512]{1,0:T(2,128)}, f32[2,512]{1,0:T(2,128)}) custom-call(f32[512,1536]{1,0:T(8,128)} %copy-done, f32[512,1536]{1,0:T(8,128)} %copy-done, f32[512,1536]{1,0:T(8,128)} %copy-done, f32[2,512]{1,0:T(2,128)} %copy-done.62, ...), custom_call_target="tpu_custom_call" | custom-call | flops 1610612736 | bytes 6291456 | tf_op jit(solution)/shard_map/attend_back/pallas_call | solution.py:606
  740.4 29.3 %all-to-all-done.1 = f32[32,16,128]{2,1,0:T(8,128)} async-done(((f32[32,16,128]{2,1,0:T(8,128)}), f32[32,16,128]{2,1,0:T(8,128)}, u32[]{:S(2)}, u32[]{:S(2)}) %all-to-all-start.1) | async-done | bytes 262176 | tf_op jit(solution)/shard_map/all_to_all | solution.py:822
  817.3 48.3 %collective-permute-done.40.refs_2_ = bf16[256,3072]{1,0:T(8,128)(2,1)} collective-permute-done((bf16[256,3072]{1,0:T(8,128)(2,1)}, bf16[256,3072]{1,0:T(8,128)(2,1)}, u32[]{:S(2)}, u32[]{:S(2)}) %collective-permute-start.40) | collective-permute-done | bytes 1572896 | tf_op jit(solution)/shard_map/ppermute | solution.py:57
  (456 shorter events, 365.5 us)
Async XLA Ops:
  7.2 86.7 %all-gather.7.cloned.1.call-start = ((), (), s32[]{:S(2)}) async-start(), calls=%async_computation.8 | async-start | bytes 7077888 | tf_op jit(solution)/shard_map/all_gather | solution.py:681
  29.1 94.1 %all-gather.9.cloned.1.call-start = ((), (), s32[]{:S(2)}) async-start(), calls=%async_computation.9 | async-start | bytes 2359296 | tf_op jit(solution)/shard_map/all_gather | solution.py:682
  29.9 296.2 %all-gather.13.cloned.1.call-start = ((), (), s32[]{:S(2)}) async-start(), calls=%async_computation.15 | async-start | bytes 4718592 | tf_op jit(solution)/shard_map/all_gather | solution.py:744
  30.6 311.1 %all-gather.11.cloned.1.call-start = ((), (), s32[]{:S(2)}) async-start(), calls=%async_computation.10 | async-start | bytes 4718592 | tf_op jit(solution)/shard_map/all_gather | solution.py:775
  156.6 446.9 %reduce-scatter.5.cloned.1.call-start = ((), (), s32[]{:S(2)}) async-start(), calls=%async_computation.11 | async-start | bytes 5013504 | tf_op jit(solution)/shard_map/reduce_scatter | solution.py:786
  181.1 100.7 %collective-permute-start.12 = (bf16[256,3072]{1,0:T(8,128)(2,1)}, bf16[256,3072]{1,0:T(8,128)(2,1)}, u32[]{:S(2)}, u32[]{:S(2)}) collective-permute-start(bf16[256,3072]{1,0:T(8,128)(2,1)} %get-tuple-element.153), channel_id=1, source_target_pairs={{0,16},{8,24},{16,0},{24,8},{1,17},{9,25},{17,1},{25,9},{2,18},{10... | collective-permute-start | bytes 4718600 | tf_op jit(solution)/shard_map/ppermute | solution.py:57
  181.7 133.8 %collective-permute-start.11 = (bf16[256,3072]{1,0:T(8,128)(2,1)}, bf16[256,3072]{1,0:T(8,128)(2,1)}, u32[]{:S(2)}, u32[]{:S(2)}) collective-permute-start(bf16[256,3072]{1,0:T(8,128)(2,1)} %get-tuple-element.154), channel_id=1, source_target_pairs={{0,16},{8,24},{16,0},{24,8},{1,17},{9,25},{17,1},{25,9},{2,18},{10... | collective-permute-start | bytes 4718600 | tf_op jit(solution)/shard_map/ppermute | solution.py:57
  183.2 132.3 %collective-permute-start.10 = (bf16[256,3072]{1,0:T(8,128)(2,1)}, bf16[256,3072]{1,0:T(8,128)(2,1)}, u32[]{:S(2)}, u32[]{:S(2)}) collective-permute-start(bf16[256,3072]{1,0:T(8,128)(2,1)} %get-tuple-element.155), channel_id=1, source_target_pairs={{0,8},{8,0},{16,24},{24,16},{1,9},{9,1},{17,25},{25,17},{2,10},{10... | collective-permute-start | bytes 4718600 | tf_op jit(solution)/shard_map/ppermute | solution.py:57
  217.6 97.9 %collective-permute-start.9 = (bf16[256,3072]{1,0:T(8,128)(2,1)}, bf16[256,3072]{1,0:T(8,128)(2,1)}, u32[]{:S(2)}, u32[]{:S(2)}) collective-permute-start(bf16[256,3072]{1,0:T(8,128)(2,1)} %get-tuple-element.156), channel_id=1, source_target_pairs={{0,8},{8,0},{16,24},{24,16},{1,9},{9,1},{17,25},{25,17},{2,10},{10... | collective-permute-start | bytes 4718600 | tf_op jit(solution)/shard_map/ppermute | solution.py:57
  330.9 150.1 %collective-permute-start.16 = (bf16[272,2048]{1,0:T(8,128)(2,1)}, bf16[272,2048]{1,0:T(8,128)(2,1)}, u32[]{:S(2)}, u32[]{:S(2)}) collective-permute-start(bf16[272,2048]{1,0:T(8,128)(2,1)} %fusion.14), channel_id=1, source_target_pairs={{0,8},{8,0},{16,24},{24,16},{1,9},{9,1},{17,25},{25,17},{2,10},{10... | collective-permute-start | bytes 3342344 | tf_op jit(solution)/shard_map/ppermute | solution.py:57
  337.8 88.4 %collective-permute-start.19 = (bf16[272,2048]{1,0:T(8,128)(2,1)}, bf16[272,2048]{1,0:T(8,128)(2,1)S(1)}, u32[]{:S(2)}, u32[]{:S(2)}) collective-permute-start(bf16[272,2048]{1,0:T(8,128)(2,1)} %fusion.17), channel_id=1, source_target_pairs={{0,16},{8,24},{16,0},{24,8},{1,17},{9,25},{17,1},{25,9},{2,18},{10... | collective-permute-start | bytes 3342344 | tf_op jit(solution)/shard_map/ppermute | solution.py:57
  346.3 114.6 %collective-permute-start.18 = (bf16[272,2048]{1,0:T(8,128)(2,1)}, bf16[272,2048]{1,0:T(8,128)(2,1)S(1)}, u32[]{:S(2)}, u32[]{:S(2)}) collective-permute-start(bf16[272,2048]{1,0:T(8,128)(2,1)} %convolution_convert_fusion.3), channel_id=1, source_target_pairs={{0,16},{8,24},{16,0},{24,8},{1,17},{9,25},{17,1},{25,9},{2,18},{10... | collective-permute-start | bytes 3342344 | tf_op jit(solution)/shard_map/ppermute | solution.py:57
  382.6 98.4 %collective-permute-start.15 = (bf16[272,2048]{1,0:T(8,128)(2,1)}, bf16[272,2048]{1,0:T(8,128)(2,1)S(1)}, u32[]{:S(2)}, u32[]{:S(2)}) collective-permute-start(bf16[272,2048]{1,0:T(8,128)(2,1)} %convolution_convert_fusion.4), channel_id=1, source_target_pairs={{0,8},{8,0},{16,24},{24,16},{1,9},{9,1},{17,25},{25,17},{2,10},{10... | collective-permute-start | bytes 3342344 | tf_op jit(solution)/shard_map/ppermute | solution.py:57
  423.9 77.2 %collective-permute-start.23 = (bf16[272,2176]{1,0:T(8,128)(2,1)}, bf16[272,2176]{1,0:T(8,128)(2,1)S(1)}, u32[]{:S(2)}, u32[]{:S(2)}) collective-permute-start(bf16[272,2176]{1,0:T(8,128)(2,1)} %get-tuple-element.95), channel_id=1, source_target_pairs={{0,24},{8,16},{16,8},{24,0},{1,25},{9,17},{17,9},{25,1},{2,26},{10... | collective-permute-start | bytes 3551240 | tf_op jit(solution)/shard_map/ppermute | solution.py:57
  539.0 343.2 %reduce-scatter.7.cloned.1.call-start = ((), (), s32[]{:S(2)}) async-start(), calls=%async_computation.12 | async-start | bytes 4718592 | tf_op jit(solution)/shard_map/reduce_scatter | solution.py:808
  601.9 282.4 %reduce-scatter.9.cloned.1.call-start = ((), (), s32[]{:S(2)}) async-start(), calls=%async_computation.13 | async-start | bytes 7077888 | tf_op jit(solution)/shard_map/reduce_scatter | solution.py:841
  695.0 180.5 %collective-permute-start.38 = (bf16[256,3072]{1,0:T(8,128)(2,1)}, bf16[256,3072]{1,0:T(8,128)(2,1)}, u32[]{:S(2)}, u32[]{:S(2)}) collective-permute-start(bf16[256,3072]{1,0:T(8,128)(2,1)} %get-tuple-element.131), channel_id=1, source_target_pairs={{0,24},{8,16},{16,8},{24,0},{1,25},{9,17},{17,9},{25,1},{2,26},{10... | collective-permute-start | bytes 4718600 | tf_op jit(solution)/shard_map/ppermute | solution.py:57
  696.2 99.1 %collective-permute-start.41 = (bf16[256,3072]{1,0:T(8,128)(2,1)}, bf16[256,3072]{1,0:T(8,128)(2,1)}, u32[]{:S(2)}, u32[]{:S(2)}) collective-permute-start(bf16[256,3072]{1,0:T(8,128)(2,1)} %get-tuple-element.135), channel_id=1, source_target_pairs={{0,24},{8,16},{16,8},{24,0},{1,25},{9,17},{17,9},{25,1},{2,26},{10... | collective-permute-start | bytes 4718600 | tf_op jit(solution)/shard_map/ppermute | solution.py:57
  714.7 178.4 %reduce-scatter.11.cloned.1.call-start = ((), (), s32[]{:S(2)}) async-start(), calls=%async_computation.14 | async-start | bytes 2359296 | tf_op jit(solution)/shard_map/reduce_scatter | solution.py:829
  780.2 95.3 %collective-permute-start.37 = (bf16[256,3072]{1,0:T(8,128)(2,1)}, bf16[256,3072]{1,0:T(8,128)(2,1)}, u32[]{:S(2)}, u32[]{:S(2)}) collective-permute-start(bf16[256,3072]{1,0:T(8,128)(2,1)} %get-tuple-element.130), channel_id=1, source_target_pairs={{0,16},{8,24},{16,0},{24,8},{1,17},{9,25},{17,1},{25,9},{2,18},{10... | collective-permute-start | bytes 4718600 | tf_op jit(solution)/shard_map/ppermute | solution.py:57
  790.2 75.4 %collective-permute-start.40 = (bf16[256,3072]{1,0:T(8,128)(2,1)}, bf16[256,3072]{1,0:T(8,128)(2,1)}, u32[]{:S(2)}, u32[]{:S(2)}) collective-permute-start(bf16[256,3072]{1,0:T(8,128)(2,1)} %get-tuple-element.134), channel_id=1, source_target_pairs={{0,16},{8,24},{16,0},{24,8},{1,17},{9,25},{17,1},{25,9},{2,18},{10... | collective-permute-start | bytes 4718600 | tf_op jit(solution)/shard_map/ppermute | solution.py:57
  790.9 84.7 %collective-permute-start.36 = (bf16[256,3072]{1,0:T(8,128)(2,1)}, bf16[256,3072]{1,0:T(8,128)(2,1)}, u32[]{:S(2)}, u32[]{:S(2)}) collective-permute-start(bf16[256,3072]{1,0:T(8,128)(2,1)} %get-tuple-element.129), channel_id=1, source_target_pairs={{0,8},{8,0},{16,24},{24,16},{1,9},{9,1},{17,25},{25,17},{2,10},{10... | collective-permute-start | bytes 4718600 | tf_op jit(solution)/shard_map/ppermute | solution.py:57
  795.3 72.1 %collective-permute-start.39 = (bf16[256,3072]{1,0:T(8,128)(2,1)}, bf16[256,3072]{1,0:T(8,128)(2,1)}, u32[]{:S(2)}, u32[]{:S(2)}) collective-permute-start(bf16[256,3072]{1,0:T(8,128)(2,1)} %get-tuple-element.133), channel_id=1, source_target_pairs={{0,8},{8,0},{16,24},{24,16},{1,9},{9,1},{17,25},{25,17},{2,10},{10... | collective-permute-start | bytes 4718600 | tf_op jit(solution)/shard_map/ppermute | solution.py:57
  797.2 87.1 %all-to-all-start.2 = ((f32[32,56,128]{2,1,0:T(8,128)}), f32[32,56,128]{2,1,0:T(8,128)}, u32[]{:S(2)}, u32[]{:S(2)}) async-start(f32[32,56,128]{2,1,0:T(8,128)} %broadcast_in_dim.18), calls=%async_computation.4 | async-start | bytes 1835008 | tf_op jit(solution)/shard_map/all_to_all | solution.py:866
  (158 other events, 2243.1 us)
Sparse Core Ops, SparseCore 0:
  29.2 64.5 all-gather.6
  95.5 27.6 all-gather.8
  124.8 46.2 all-gather.12
  173.1 45.6 all-gather.10
  539.1 51.6 reduce-scatter.4
  602.0 48.7 reduce-scatter.6
  676.5 72.5 reduce-scatter.8
  751.5 35.3 reduce-scatter.10

commit v2 on v1

--- a/solution.py
+++ b/solution.py
@@ -14,7 +14,9 @@
 neg_large = -1e30
 f32 = jnp.float32
 bf16 = jnp.bfloat16
-everyone = ("fsdp", "ctx")
+CTX = "ctx"
+FSDP = "fsdp"
+everyone = (FSDP, CTX)
 
 
 def mm(a, b):
@@ -54,48 +56,66 @@
 
 
 def from_peer(values, offset, total):
-    return lax.ppermute(values, "ctx", [(i, i ^ offset) for i in range(total)])
-
-
-def place_kernel(order, rows, block, place_ref, *refs):
+    return lax.ppermute(values, CTX, [(i, i ^ offset) for i in range(total)])
+
+
+def place_kernel(order, total, place_ref, *refs):
     parts, whole, sems = refs[:-2], refs[-2], refs[-1]
     step = pl.program_id(0)
-    copies = []
-    for n, (j, half) in enumerate(order):
-        first = ((place_ref[0] ^ j) * 2 + half) * rows + step * block
-        first = pl.multiple_of(first, block)
-        copies.append(
-            pltpu.make_async_copy(parts[n], whole.at[pl.ds(first, block), :], sems.at[n])
-        )
-        copies[-1].start()
-    for copy in copies:
-        copy.wait()
-
-
-def place_parts(place, order, parts):
-    rows, width = parts[0].shape
-    block = min(64, rows)
-    steps = rows // block
+
+    def copy(n):
+        j, begin, rows = order[n]
+        block = min(64, rows)
+        first = pl.multiple_of((place_ref[0] ^ j) * total + begin + step * block, block)
+        part = parts[n].at[0] if j == 0 else parts[n]
+        return pltpu.make_async_copy(part, whole.at[pl.ds(first, block), :], sems.at[n])
+
+    for n in range(len(parts)):
+
+        @pl.when(step < order[n][2] // min(64, order[n][2]))
+        def _():
+            copy(n).start()
+
+    for n in range(len(parts)):
+
+        @pl.when(step < order[n][2] // min(64, order[n][2]))
+        def _():
+            copy(n).wait()
+
+
+def place_parts(place, pieces, order, parts, total):
+    width = parts[0].shape[-1]
+    places = max(o[0] for o in order) + 1
+
+    def spec(j, begin, rows):
+        block = min(64, rows)
+        last = rows // block - 1
+        if j == 0:
+            return pl.BlockSpec(
+                (1, block, width),
+                lambda i, s: (s[0] // pieces, begin // block + jnp.minimum(i, last), 0),
+            )
+        return pl.BlockSpec((block, width), lambda i, s: (jnp.minimum(i, last), 0))
+
     return pl.pallas_call(
-        functools.partial(place_kernel, order, rows, block),
+        functools.partial(place_kernel, order, total),
         grid_spec=pltpu.PrefetchScalarGridSpec(
             num_scalar_prefetch=1,
-            grid=(steps,),
-            in_specs=[pl.BlockSpec((block, width), lambda i, s: (i, 0))] * len(parts),
+            grid=(max(o[2] // min(64, o[2]) for o in order),),
+            in_specs=[spec(*o) for o in order],
             out_specs=pl.BlockSpec(memory_space=pl.ANY),
             scratch_shapes=[pltpu.SemaphoreType.DMA((len(parts),))],
         ),
-        out_shape=jax.ShapeDtypeStruct((len(parts) * rows, width), parts[0].dtype),
-        compiler_params=pltpu.CompilerParams(vmem_limit_bytes=30 << 20),
+        out_shape=jax.ShapeDtypeStruct((places * total, width), bf16),
+        compiler_params=pltpu.CompilerParams(vmem_limit_bytes=40 << 20),
         cost_estimate=pl.CostEstimate(
-            flops=0, bytes_accessed=4 * len(parts) * rows * width, transcendentals=0
-        ),
-        name="place_parts",
+            flops=0, bytes_accessed=4 * places * total * width, transcendentals=0
+        ),
     )(place, *parts)
 
 
 def merge_kernel(steps, block, total, pieces, base, place_ref, *refs):
-    parts, whole, held, sems = refs[: total * pieces], refs[-3], refs[-2], refs[-1]
+    whole, held, sems = refs[-3], refs[-2], refs[-1]
     step = pl.program_id(0)
     slot = lax.rem(step, 2)
 
@@ -105,38 +125,49 @@
             held.at[side, m], whole.at[rows, place_ref[0] ^ m, :], sems.at[side, m]
         )
 
+    def widen(m, which):
+        value = refs[2 * m * pieces + which][...].astype(f32)
+        for p in range(1, pieces):
+            value = value + refs[2 * (m * pieces + p) + which][...].astype(f32)
+        held[slot, m] = value
+
     for m in range(total):
 
         @pl.when(step >= 2)
         def _():
             copy(step - 2, slot, m).wait()
 
-        value = parts[m * pieces][...].astype(f32)
-        for p in range(1, pieces):
-            value = value + parts[m * pieces + p][...].astype(f32)
-        held[slot, m] = value
+        @pl.when(step < steps // 2)
+        def _():
+            widen(m, 0)
+
+        @pl.when(step >= steps // 2)
+        def _():
+            widen(m, 1)
+
         copy(step, slot, m).start()
 
     @pl.when(step == steps - 1)
     def _():
         for m in range(total):
-            if steps >= 2:
-                copy(step - 1, 1 - slot, m).wait()
+            copy(step - 1, 1 - slot, m).wait()
             copy(step, slot, m).wait()
 
 
 def merge_parts(place, parts, total, base, rows_total, whole=None):
     rows, width = parts[0].shape
-    pieces = len(parts) // total
+    pieces = len(parts) // (2 * total)
     block = min(64, rows)
-    steps = rows // block
+    steps = 2 * rows // block
     more = [] if whole is None else [whole]
+    upper = pl.BlockSpec((block, width), lambda i, s: (jnp.minimum(i, steps // 2 - 1), 0))
+    lower = pl.BlockSpec((block, width), lambda i, s: (jnp.maximum(i - steps // 2, 0), 0))
     return pl.pallas_call(
         functools.partial(merge_kernel, steps, block, total, pieces, base),
         grid_spec=pltpu.PrefetchScalarGridSpec(
             num_scalar_prefetch=1,
             grid=(steps,),
-            in_specs=[pl.BlockSpec((block, width), lambda i, s: (i, 0))] * len(parts)
+            in_specs=[upper, lower] * (len(parts) // 2)
             + [pl.BlockSpec(memory_space=pl.ANY)] * len(more),
             out_specs=pl.BlockSpec(memory_space=pl.ANY),
             scratch_shapes=[
@@ -146,13 +177,12 @@
         ),
         out_shape=jax.ShapeDtypeStruct((rows_total, total, width), f32),
         input_output_aliases={1 + len(parts): 0} if more else {},
-        compiler_params=pltpu.CompilerParams(vmem_limit_bytes=30 << 20),
+        compiler_params=pltpu.CompilerParams(vmem_limit_bytes=36 << 20),
         cost_estimate=pl.CostEstimate(
             flops=0,
-            bytes_accessed=2 * len(parts) * rows * width + 4 * total * rows * width,
+            bytes_accessed=2 * len(parts) * rows * width + 8 * total * rows * width,
             transcendentals=0,
         ),
-        name="merge_parts",
     )(place, *parts, *more)
 
 
@@ -316,32 +346,43 @@
             bytes_accessed=6 * width * ff + 10 * count * width,
             transcendentals=count * ff,
         ),
-        name="expert",
     )(mine, rows, cots, router, expert, expert, expert)
 
 
 def weight_kernel(groups, steps, place_ref, *refs):
     step = pl.program_id(0)
-
-    def total(left, right):
-        result = mm_tn(refs[left][...], refs[right][...])
-        for g in range(1, groups):
-            result = result + mm_tn(refs[5 * g + left][...], refs[5 * g + right][...])
-        half = refs[-1].shape[0]
-        refs[-2][...] = result[:half].astype(bf16)
-        refs[-1][...] = result[half:].astype(bf16)
+    outs = refs[5 * groups : 5 * groups + 4]
+    left, right = refs[-2], refs[-1]
+    count = refs[0].shape[0]
+
+    def gather(into, which):
+        for g in range(groups):
+            into[g * count : (g + 1) * count, :] = refs[5 * g + which][...]
+
+    @pl.when(step == 0)
+    def _():
+        gather(left, 0)
+
+    @pl.when(step == 2 * steps)
+    def _():
+        gather(left, 1)
 
     @pl.when(step < steps)
     def _():
-        total(0, 2)
+        gather(right, 2)
 
     @pl.when((step >= steps) & (step < 2 * steps))
     def _():
-        total(0, 3)
+        gather(right, 3)
 
     @pl.when(step >= 2 * steps)
     def _():
-        total(1, 4)
+        gather(right, 4)
+
+    result = mm_tn(left[...], right[...]).astype(bf16)
+    rows = outs[0].shape[0]
+    for n, out_ref in enumerate(outs):
+        out_ref[...] = result[n * rows : (n + 1) * rows]
 
 
 def weight_grad(place, groups, columns):
@@ -363,45 +404,49 @@
             num_scalar_prefetch=1,
             grid=(3 * steps,),
             in_specs=[side, side, part(0), part(1), part(2)] * len(groups),
-            out_specs=[pl.BlockSpec((columns // 2, block), lambda i, s: (0, i))] * 2,
-        ),
-        out_shape=[jax.ShapeDtypeStruct((columns // 2, 3 * ff), bf16)] * 2,
+            out_specs=[pl.BlockSpec((columns // 4, block), lambda i, s: (0, i))] * 4,
+            scratch_shapes=[
+                pltpu.VMEM((len(groups) * count, columns), bf16),
+                pltpu.VMEM((len(groups) * count, block), bf16),
+            ],
+        ),
+        out_shape=[jax.ShapeDtypeStruct((columns // 4, 3 * ff), bf16)] * 4,
         compiler_params=pltpu.CompilerParams(vmem_limit_bytes=48 << 20),
         cost_estimate=pl.CostEstimate(
             flops=6 * len(groups) * count * columns * ff,
             bytes_accessed=6 * columns * ff + 10 * len(groups) * count * ff,
             transcendentals=0,
         ),
-        name="weight_grad",
     )(place, *[a for group in groups for a in group])
 
 
 def collect_kernel(total, *refs):
-    result = dot_nn(refs[0][...], refs[total][...])
-    for j in range(1, total):
-        result = result + dot_nn(refs[j][...], refs[total + j][...])
-    refs[-1][...] = result.astype(bf16)
+    places, parts, out_ref, rows = refs[0], refs[1 : 1 + total], refs[-2], refs[-1]
+    count = parts[0].shape[0]
+    for j in range(total):
+        rows[j * count : (j + 1) * count, :] = parts[j][...]
+    out_ref[...] = dot_nn(places[...], rows[...]).astype(bf16)
 
 
 def collect_rows(places, parts):
-    tokens = places[0].shape[0]
+    tokens, count = places.shape
     rows, width = parts[0].shape
     block = 512 if width % 512 == 0 else 768
     return pl.pallas_call(
         functools.partial(collect_kernel, len(parts)),
         grid=(pl.cdiv(width, block),),
-        in_specs=[pl.BlockSpec((tokens, rows), lambda i: (0, 0))] * len(parts)
+        in_specs=[pl.BlockSpec((tokens, count), lambda i: (0, 0))]
         + [pl.BlockSpec((rows, block), lambda i: (0, i))] * len(parts),
         out_specs=pl.BlockSpec((tokens, block), lambda i: (0, i)),
         out_shape=jax.ShapeDtypeStruct((tokens, width), bf16),
+        scratch_shapes=[pltpu.VMEM((count, block), bf16)],
         compiler_params=pltpu.CompilerParams(vmem_limit_bytes=48 << 20),
         cost_estimate=pl.CostEstimate(
-            flops=2 * len(parts) * tokens * rows * width,
-            bytes_accessed=2 * len(parts) * rows * (width + tokens) + 2 * tokens * width,
+            flops=2 * tokens * count * width,
+            bytes_accessed=2 * count * (width + tokens) + 2 * tokens * width,
             transcendentals=0,
         ),
-        name="collect_rows",
-    )(*places, *parts)
+    )(places, *parts)
 
 
 def turn(values, cosine, sine):
@@ -550,7 +595,6 @@
         cost_estimate=pl.CostEstimate(
             flops=16 * seq * width, bytes_accessed=26 * seq * width, transcendentals=0
         ),
-        name="finish",
     )(yq, yk, gv, raw_qkv, gains, scales, *parts)
 
 
@@ -595,7 +639,6 @@
             bytes_accessed=12 * seq * width,
             transcendentals=seq * seq * heads,
         ),
-        name="attend",
     )(raw_qkv, raw_qkv, raw_qkv, *tables, *parts)
 
 
@@ -622,7 +665,6 @@
             bytes_accessed=24 * seq * width,
             transcendentals=seq * seq * heads,
         ),
-        name="attend_back",
     )(raw_qkv, raw_qkv, raw_qkv, *tables, scales, grad)
 
 
@@ -649,8 +691,8 @@
     local_experts = experts.shape[1]
     top_count = routes.shape[2]
     ff = experts.shape[2] // 3
-    C = lax.axis_size("ctx")
-    F = lax.axis_size("fsdp")
+    C = lax.axis_size(CTX)
+    F = lax.axis_size(FSDP)
     devices = C * F
     W = model_width // C
     seq = C * row_total
@@ -658,46 +700,55 @@
     pieces = C // local_experts
     cap_unit = 16 * expert_total * pieces
     piece_cap = (17 * row_total * top_count + cap_unit - 1) // cap_unit
-    me = lax.axis_index("ctx")
-    row = lax.axis_index("fsdp")
+    me = lax.axis_index(CTX)
+    row = lax.axis_index(FSDP)
     my_expert = row * local_experts + me // pieces
     my_column = me * W
 
     tokens_low = tokens.reshape(row_total, model_width)
     tokens_seq = gather_rows(tokens_low, C)
     route_ids = routes.reshape(row_total, top_count)
-    column_ids = lax.all_gather(route_ids, "fsdp", axis=0, tiled=True)
+    column_ids = lax.all_gather(route_ids, FSDP, axis=0, tiled=True)
 
     def by_column(weight):
         return jnp.swapaxes(weight.reshape(shard, C, W), 0, 1)
 
     w_cols = lax.all_to_all(
         jnp.concatenate([by_column(w_query), by_column(w_key), by_column(w_value)], 2),
-        "ctx",
+        CTX,
         split_axis=0,
         concat_axis=0,
         tiled=True,
     )
-    w_qkv = lax.all_gather(w_cols, "fsdp", axis=1, tiled=True).reshape(model_width, 3 * W)
-    w_o = lax.all_gather(output_weight, "fsdp", axis=0, tiled=True)
+    w_qkv = lax.all_gather(w_cols, FSDP, axis=1, tiled=True).reshape(model_width, 3 * W)
+    w_o = lax.all_gather(output_weight, FSDP, axis=0, tiled=True)
 
     by_expert = lax.optimization_barrier(
         jnp.swapaxes(lax.optimization_barrier(experts), 0, 1)
     )
     half = slice_rows // 2
-    own = []
-    order = []
-    for j in range(C):
-        for part in range(2):
-            piece = lax.dynamic_slice(
-                by_expert, ((me ^ j) // pieces, part * half, 0), (1, half, 3 * ff)
-            ).reshape(half, 3 * ff)
-            order.append((j, part))
-            if j == 0:
-                own.append(piece)
-            else:
-                own.append(from_peer(piece, j, C))
-    expert = place_parts(me.reshape(1), order, own)
+
+    def expert_slice(array, j, begin, rows):
+        first = ((me ^ j) // pieces, begin, 0)
+        return lax.dynamic_slice(array, first, (1, rows, 3 * ff)).reshape(rows, 3 * ff)
+
+    near = [j for j in range(1, C) if j & (j - 1) == 0]
+    far = [j for j in range(1, C) if j not in near]
+    eighth = slice_rows // 8
+    near_cuts = [(j, part * half, half) for part in range(2) for j in near]
+    far_cuts = [(j, part * eighth, eighth) for part in range(8) for j in far]
+    cut = [expert_slice(by_expert, *o) for o in near_cuts]
+    cut, later_expert = lax.optimization_barrier((cut, by_expert))
+    own = [later_expert] * 2
+    order = [(0, 0, half), (0, half, half)]
+    for o, piece in zip(near_cuts, cut):
+        order.append(o)
+        own.append(from_peer(piece, o[0], C))
+    for o in far_cuts:
+        order.append(o)
+        piece = expert_slice(later_expert, *o)
+        own.append(from_peer(piece, o[0], C))
+    expert = place_parts(me.reshape(1), pieces, tuple(order), own, slice_rows)
 
     column_rows = F * row_total
     member = jnp.sum(
@@ -735,13 +786,14 @@
         return result
 
     def deliver(values):
-        return exchange([mm(select, values).astype(bf16) for select in selects])
+        parts = [mm(select, values).astype(bf16) for select in selects]
+        return exchange(parts)
 
     def collect(parts):
         return collect_rows(places, parts)
 
     cot_low = cotangent.reshape(row_total, model_width)
-    cot_column = lax.all_gather(cot_low, "fsdp", axis=0, tiled=True)
+    cot_column = lax.all_gather(cot_low, FSDP, axis=0, tiled=True)
     cot_rows = deliver(cot_column)
 
     place = me ^ jnp.arange(C, dtype=jnp.int32)
@@ -758,6 +810,7 @@
     scale_one = inv_rms(inputs_seq)
     normed = (inputs_seq * scale_one * attn_gain).astype(bf16)
     gains = lax.dynamic_slice_in_dim(jnp.stack([query_gain, key_gain]), my_column, W, 1)
+    places = jnp.concatenate(places, 1)
     w_qkv, selects, places = lax.optimization_barrier((w_qkv, selects, places))
     raw_qkv = mm(normed, w_qkv)
     raw_q = raw_qkv[:, :W]
@@ -772,7 +825,7 @@
     scale_two = inv_rms(hidden_one)
     ffn_in = (hidden_one * scale_two * ffn_gain).astype(bf16)
     probs = jax.nn.softmax(mm(ffn_in, router), -1)
-    ffn_column = lax.all_gather(ffn_in, "fsdp", axis=0, tiled=True)
+    ffn_column = lax.all_gather(ffn_in, FSDP, axis=0, tiled=True)
     expert_in = deliver(ffn_column)
     extra = -(-2 * expert_total // 128) * 128
     done = []
@@ -783,29 +836,30 @@
             result, mine = lax.optimization_barrier((result, mine))
         done.append(result)
     back = collect(exchange([d[0] for d in done]))
-    back = lax.psum_scatter(back, "fsdp", scatter_dimension=0, tiled=True).astype(f32)
+    back = lax.psum_scatter(back, FSDP, scatter_dimension=0, tiled=True).astype(f32)
     groups = [(expert_in[j], done[j][2], done[j][3], done[j][4], done[j][5]) for j in range(C)]
     d_own = []
     for j in range(C):
         d_own.append(weight_grad((me ^ j).reshape(1), groups, slice_rows))
+    arrived = {}
+    for j in range(C):
+        for part in range(4):
+            if j == 0:
+                arrived[j, part] = d_own[j][part]
+            else:
+                arrived[j, part] = from_peer(d_own[j][part], j, C)
     d_experts = None
     for part in range(2):
-        pieces_here = []
-        for j in range(C):
-            if j == 0:
-                pieces_here.append(d_own[j][part])
-            else:
-                pieces_here.append(from_peer(d_own[j][part], j, C))
         d_experts = merge_parts(
             (me // pieces).reshape(1),
-            pieces_here,
+            [arrived[j, 2 * part + n] for j in range(C) for n in range(2)],
             local_experts,
             part * half,
             slice_rows,
             d_experts,
         )
     mixed = collect(exchange([d[1] for d in done]))
-    mixed = lax.psum_scatter(mixed, "fsdp", scatter_dimension=0, tiled=True).astype(f32)
+    mixed = lax.psum_scatter(mixed, FSDP, scatter_dimension=0, tiled=True).astype(f32)
 
     grad_probs = (
         back[:, model_width : model_width + expert_total]
@@ -818,17 +872,23 @@
     grad_router = mm_tn(grad_logits, ffn_in)
     grad_hidden_one, grad_ffn_gain = norm_back(grad_ffn, hidden_one, scale_two, ffn_gain)
     grad_hidden_one = grad_hidden_one + cot_low.astype(f32)
-    router_slice = jnp.sum(
-        lax.all_to_all(grad_router.reshape(devices, -1, 128), everyone, 0, 0, tiled=True), 0
-    )
+    share = model_width // devices
+    sums = jnp.concatenate(
+        [grad_router.reshape(devices, -1), grad_ffn_gain.reshape(devices, share)], 1
+    )
+    sums = jnp.sum(lax.all_to_all(sums[:, None], everyone, 0, 0, tiled=True), 0)
+    sums = lax.all_to_all(
+        jnp.broadcast_to(sums, (devices,) + sums.shape), everyone, 0, 0, tiled=True
+    ).reshape(devices, -1)
+    d_ffn_gain = sums[:, -share:].reshape(model_width)
+    d_router = sums[:, :-share].reshape(expert_total, model_width).T
 
     branch_seq = gather_rows(grad_hidden_one.astype(bf16), C)
+    grad_att = mm_nt(branch_seq, w_o).astype(bf16)
     d_output = mm_tn(attended, branch_seq).astype(bf16)
-    grad_att = mm_nt(branch_seq, w_o).astype(bf16)
     grad_att, d_output = lax.optimization_barrier((grad_att, d_output))
-    d_output = lax.psum_scatter(
-        d_output, "fsdp", scatter_dimension=0, tiled=True
-    ).astype(f32)
+
+    d_output = lax.psum_scatter(d_output, FSDP, scatter_dimension=0, tiled=True).astype(f32)
     grad_q_n, grad_k_n, grad_value, dots, gain_grads = attend_back(
         raw_qkv, tables, scales, grad_att
     )
@@ -840,13 +900,20 @@
     )
     d_cols = lax.psum_scatter(
         mm_tn(normed, grad_qkv).astype(bf16).reshape(C, F * shard, 3 * W),
-        "fsdp",
+        FSDP,
         scatter_dimension=1,
         tiled=True,
     )
-    d_cols = lax.all_to_all(d_cols, "ctx", 0, 0, tiled=True).reshape(C, shard, 3, W)
+    received = []
+    for j in range(C):
+        piece = lax.dynamic_index_in_dim(d_cols, me ^ j, 0, keepdims=False)
+        received.append(from_peer(piece, j, C) if j else piece)
+    received = jnp.stack(received)
+    received = [
+        lax.dynamic_index_in_dim(received, me ^ c, 0, keepdims=False) for c in range(C)
+    ]
     d_qkv = [
-        jnp.swapaxes(d_cols[:, :, n], 0, 1).reshape(shard, model_width).astype(f32)
+        jnp.concatenate([r[:, n * W : (n + 1) * W] for r in received], 1).astype(f32)
         for n in range(3)
     ]
 
@@ -854,26 +921,14 @@
     grad_inputs, grad_attn_gain = norm_back(grad_normed, inputs, scale_one[:row_total], attn_gain)
     grad_inputs = grad_inputs + grad_hidden_one
 
-    vector = jnp.concatenate(
-        [
-            grad_attn_gain,
-            grad_ffn_gain,
-            gain_grads[0],
-            gain_grads[1],
-            router_slice.reshape(-1),
-        ]
-    ).reshape(1, -1, 128)
+    vector = jnp.concatenate([grad_attn_gain, gain_grads[0], gain_grads[1]]).reshape(1, -1, 128)
     everything = lax.all_to_all(
         jnp.broadcast_to(vector, (devices,) + vector.shape[1:]), everyone, 0, 0, tiled=True
     ).reshape(devices, -1)
     d_attn_gain = jnp.sum(everything[:, :model_width], 0)
-    d_ffn_gain = jnp.sum(everything[:, model_width : 2 * model_width], 0)
-    by_place = jnp.sum(
-        everything[:, 2 * model_width : 2 * model_width + 2 * W].reshape(F, C, 2, W), 0
-    )
+    by_place = jnp.sum(everything[:, model_width:].reshape(F, C, 2, W), 0)
     d_query_gain = by_place[:, 0].reshape(model_width)
     d_key_gain = by_place[:, 1].reshape(model_width)
-    d_router = everything[:, 2 * model_width + 2 * W :].reshape(expert_total, model_width).T
 
     return (
         output,
@@ -893,37 +948,37 @@
 
 def solution(mesh):
     placed = (
-        P("fsdp", "ctx", None),
+        P(FSDP, CTX, None),
         P(),
         P(),
         P(),
-        P(("ctx", "fsdp"), None),
-        P(("ctx", "fsdp"), None),
-        P(("ctx", "fsdp"), None),
-        P(("ctx", "fsdp"), None),
+        P((CTX, FSDP), None),
+        P((CTX, FSDP), None),
+        P((CTX, FSDP), None),
+        P((CTX, FSDP), None),
         P(),
         P(),
-        P("ctx", "fsdp", None),
-        P("fsdp", "ctx", None),
-        P("fsdp", "ctx", None),
+        P(CTX, FSDP, None),
+        P(FSDP, CTX, None),
+        P(FSDP, CTX, None),
     )
     return jax.shard_map(
         layer,
         mesh=mesh,
         in_specs=placed,
         out_specs=(
-            P("fsdp", "ctx", None),
-            P("fsdp", "ctx", None),
+            P(FSDP, CTX, None),
+            P(FSDP, CTX, None),
             P(),
             P(),
             P(),
-            P(("ctx", "fsdp"), None),
-            P(("ctx", "fsdp"), None),
-            P(("ctx", "fsdp"), None),
-            P(("ctx", "fsdp"), None),
+            P((CTX, FSDP), None),
+            P((CTX, FSDP), None),
+            P((CTX, FSDP), None),
+            P((CTX, FSDP), None),
             P(),
             P(),
-            P("ctx", "fsdp", None),
+            P(CTX, FSDP, None),
         ),
         check_vma=False,
     )

time: 913 us -> 924 us (1.012)
  starting transfers between devices: 64.8 us -> 85.8 us
  Pallas kernels: 174 us -> 161 us
  waiting for transfers between devices: 460 us -> 448 us
  local copies, waits for them, and re-layouts: 83.3 us -> 94.8 us
    all_to_all x2, waiting for transfers between devices: 31.5 us -> 0.01 us  [the longest x1 0.01 us: layer(): lax.all_to_all(jnp.broadcast_to(sums, (devices,) + sums.shape), everyone,...]
    ppermute x42 -> x57, starting transfers between devices: 53.4 us -> 73 us  [from_peer(): return lax.ppermute(values, CTX, [(i, i ^ offset) for i in range(total)])]
    ppermute x42 -> x57, waiting for transfers between devices: 387 us -> 401 us  [from_peer(): return lax.ppermute(values, CTX, [(i, i ^ offset) for i in range(total)])]
    all_to_all x1, waiting for transfers between devices: 0.01 us -> 12.2 us  [layer(): lax.all_to_all(jnp.broadcast_to(vector, (devices,) + vector.shape[1:]), e...]
    unnamed x268 -> x257, local copies, waits for them, and re-layouts: 45.8 us -> 51.8 us
  transfers between devices with their start and end apart: 53 -> 68, of which waited for: 30 -> 42; matrix products, arithmetic and copies ran while one was open for 12% -> 13% of each run, Pallas kernels for 18% -> 16%
where the time goes in v2:
time: 924 us; the launch traced here: 919 us
  waiting for transfers between devices  448 us (48%)
  Pallas kernels  161 us (17%)
  local copies, waits for them, and re-layouts  94.8 us (10%)
  starting transfers between devices  85.8 us (9%)
  matrix products  55.3 us (6%)
  blocking collectives  31.4 us (3%)
  other arithmetic  28 us (3%)
  between operations  15.5 us (2%)
    ppermute x57, waiting for transfers between devices, from_peer(): return lax.ppermute(values, CTX, [(i, i ^ offset) for i in range(total)])  401 us
    ppermute x57, starting transfers between devices, from_peer(): return lax.ppermute(values, CTX, [(i, i ^ offset) for i in range(total)])  73 us
    pallas_call x4, Pallas kernels, run_expert(): pl.pallas_call(functools.partial(expert_kernel, steps), grid_spec=pltpu.P...  56.7 us
    unnamed x257, local copies, waits for them, and re-layouts  51.8 us
    pallas_call x4, Pallas kernels, weight_grad(): pl.pallas_call(functools.partial(weight_kernel, len(groups), steps), grid...  37.8 us
    dot_general x11, matrix products, mm(): return jnp.dot(a, b, preferred_element_type=f32)  31.2 us
    all_gather x1, waiting for transfers between devices, layer(): lax.all_gather(w_cols, FSDP, axis=1, tiled=True).reshape(model_width, 3 * W)  29.6 us
    pallas_call x2, Pallas kernels, collect_rows(): pl.pallas_call(functools.partial(collect_kernel, len(parts)), grid=(pl.cd...  18.9 us
  transfers between devices with their start and end apart: 68, of which 42 were waited for; matrix products, arithmetic and copies ran while one was open for 13% of the time, Pallas kernels for 16%

profile of v2, /device:TPU:0, one launch (start us, length us, event | category | flops | bytes accessed | tf_op | source)
XLA Modules:
  0.0 919.0 jit_solution(8585034180237522817)
XLA Ops:
  11.2 16.5 %all_to_all.20 = bf16[4,64,1536]{2,1,0:T(8,128)(2,1)S(1)} all-to-all(bf16[4,64,1536]{2,1,0:T(8,128)(2,1)S(1)} %copy.100), channel_id=1, replica_groups=mesh['ctx'=4,'fsdp'=8] {'ctx'}, dimensions={0} | all-to-all | bytes 1572864 | tf_op jit(solution)/shard_map/all_to_all | solution.py:716
  34.2 14.9 %all-gather = s32[1,1024,8]{1,2,0:T(8,128)S(1)} all-gather(s32[1,128,8]{1,2,0:T(8,128)S(1)} %copy-done.116), channel_id=2, replica_groups=mesh['ctx'=4,'fsdp'=8] {'fsdp'}, dimensions={1}, use_global_device_ids=true | all-gather | bytes 36864 | tf_op jit(solution)/shard_map/all_gather | solution.py:711
  64.2 29.6 %all-gather.7.cloned.1.call-done = bf16[4,512,1536]{2,0,1:T(4,128)(2,1)} async-done(((bf16[4,64,1536]{2,0,1:T(4,128)(2,1)}), bf16[4,512,1536]{2,0,1:T(4,128)(2,1)}) %all-gather.7.cloned.1.call-update) | async-done | bytes 6291472 | tf_op jit(solution)/shard_map/all_gather | solution.py:723
  141.3 11.5 %collective-permute-done.8 = bf16[128,2048]{1,0:T(8,128)(2,1)S(1)} collective-permute-done((bf16[128,2048]{1,0:T(8,128)(2,1)S(1)}, bf16[128,2048]{1,0:T(8,128)(2,1)S(1)}, u32[]{:S(2)}, u32[]{:S(2)}) %collective-permute-start.8) | collective-permute-done | bytes 524320 | tf_op jit(solution)/shard_map/ppermute | solution.py:59
  157.2 13.2 %copy.131 = bf16[512,4,3072]{2,0,1:T(8,128)(2,1)} copy(bf16[512,4,3072]{2,1,0:T(4,128)(2,1)} %param.23) | data formatting | bytes 25165824 | tf_op jit(solution)/shard_map/optimization_barrier | solution.py:727
  227.9 71.6 %collective-permute-done.15.refs_8_ = bf16[64,3072]{1,0:T(8,128)(2,1)S(1)} collective-permute-done((bf16[64,3072]{1,0:T(8,128)(2,1)S(1)}, bf16[64,3072]{1,0:T(8,128)(2,1)S(1)}, u32[]{:S(2)}, u32[]{:S(2)}) %collective-permute-start.15) | collective-permute-done | bytes 393248 | tf_op jit(solution)/shard_map/ppermute | solution.py:59
  361.5 14.2 %shard_map.222 = (bf16[272,2176]{1,0:T(8,128)(2,1)}, bf16[272,2048]{1,0:T(8,128)(2,1)S(1)}, bf16[272,2048]{1,0:T(8,128)(2,1)S(1)}, bf16[272,1024]{1,0:T(8,128)(2...) custom-call(s32[1]{0:T(128)} %bitcast.19.mine_ref, ...), custom_call_target="tpu_custom_call" | custom-call | flops 6845104128 | bytes 18153472 | tf_op jit(solution)/shard_map/pallas_call | solution.py:308
  378.2 13.8 %collective-permute-done.28.cots_ref = bf16[272,2048]{1,0:T(8,128)(2,1)S(1)} collective-permute-done((bf16[272,2048]{1,0:T(8,128)(2,1)}, bf16[272,2048]{1,0:T(8,128)(2,1)S(1)}, u32[]{:S(2)}, u32[]{:S(2)}) %collective-permute-start.28) | collective-permute-done | bytes 1114144 | tf_op jit(solution)/shard_map/ppermute | solution.py:59
  393.5 22.3 %collective-permute-done.27.rows_ref.refs_15_ = bf16[272,2048]{1,0:T(8,128)(2,1)S(1)} collective-permute-done((bf16[272,2048]{1,0:T(8,128)(2,1)}, bf16[272,2048]{1,0:T(8,128)(2,1)S(1)}, u32[]{:S(2)}, u32[]{:S(2)}) %collective-permute-start.27) | collective-permute-done | bytes 1114144 | tf_op jit(solution)/shard_map/ppermute | solution.py:59
  415.9 14.2 %shard_map.225 = (bf16[272,2176]{1,0:T(8,128)(2,1)}, bf16[272,2048]{1,0:T(8,128)(2,1)S(1)}, bf16[272,2048]{1,0:T(8,128)(2,1)S(1)}, bf16[272,1024]{1,0:T(8,128)(2...) custom-call(s32[1]{0:T(128)} %bitcast.19.mine_ref, ...), custom_call_target="tpu_custom_call" | custom-call | flops 6845104128 | bytes 18153472 | tf_op jit(solution)/shard_map/pallas_call | solution.py:308
  435.7 31.1 %collective-permute-done.24.rows_ref.refs_10_ = bf16[272,2048]{1,0:T(8,128)(2,1)S(1)} collective-permute-done((bf16[272,2048]{1,0:T(8,128)(2,1)S(1)}, bf16[272,2048]{1,0:T(8,128)(2,1)S(1)}, u32[]{:S(2)}, u32[]{:S(2)}) %collective-permute-start.24) | collective-permute-done | bytes 1114144 | tf_op jit(solution)/shard_map/ppermute | solution.py:59
  466.8 14.2 %shard_map.224 = (bf16[272,2176]{1,0:T(8,128)(2,1)}, bf16[272,2048]{1,0:T(8,128)(2,1)S(1)}, bf16[272,2048]{1,0:T(8,128)(2,1)S(1)}, bf16[272,1024]{1,0:T(8,128)(2...) custom-call(s32[1]{0:T(128)} %bitcast.19.mine_ref, ...), custom_call_target="tpu_custom_call" | custom-call | flops 6845104128 | bytes 18153472 | tf_op jit(solution)/shard_map/pallas_call | solution.py:308
  485.9 14.2 %shard_map.223 = (bf16[272,2176]{1,0:T(8,128)(2,1)}, bf16[272,2048]{1,0:T(8,128)(2,1)S(1)}, bf16[272,2048]{1,0:T(8,128)(2,1)S(1)}, bf16[272,1024]{1,0:T(8,128)(2...) custom-call(s32[1]{0:T(128)} %bitcast.19.mine_ref, ...), custom_call_target="tpu_custom_call" | custom-call | flops 6845104128 | bytes 18153472 | tf_op jit(solution)/shard_map/pallas_call | solution.py:308
  507.6 19.9 %collective-permute-done.23.refs_2_ = bf16[272,2176]{1,0:T(8,128)(2,1)S(1)} collective-permute-done((bf16[272,2176]{1,0:T(8,128)(2,1)}, bf16[272,2176]{1,0:T(8,128)(2,1)S(1)}, u32[]{:S(2)}, u32[]{:S(2)}) %collective-permute-start.23) | collective-permute-done | bytes 1183776 | tf_op jit(solution)/shard_map/ppermute | solution.py:59
  541.0 24.8 %collective-permute-done.38.refs_4_ = bf16[272,2048]{1,0:T(8,128)(2,1)S(1)} collective-permute-done((bf16[272,2048]{1,0:T(8,128)(2,1)S(1)}, bf16[272,2048]{1,0:T(8,128)(2,1)S(1)}, u32[]{:S(2)}, u32[]{:S(2)}) %collective-permute-start.38) | collective-permute-done | bytes 1114144 | tf_op jit(solution)/shard_map/ppermute | solution.py:59
  565.8 16.7 %collective-permute-done.37.refs_3_ = bf16[272,2048]{1,0:T(8,128)(2,1)S(1)} collective-permute-done((bf16[272,2048]{1,0:T(8,128)(2,1)S(1)}, bf16[272,2048]{1,0:T(8,128)(2,1)S(1)}, u32[]{:S(2)}, u32[]{:S(2)}) %collective-permute-start.37) | collective-permute-done | bytes 1114144 | tf_op jit(solution)/shard_map/ppermute | solution.py:59
  600.3 12.2 %collective-permute-done.32 = bf16[128,2048]{1,0:T(8,128)(2,1)S(1)} collective-permute-done((bf16[128,2048]{1,0:T(8,128)(2,1)S(1)}, bf16[128,2048]{1,0:T(8,128)(2,1)S(1)}, u32[]{:S(2)}, u32[]{:S(2)}) %collective-permute-start.32) | collective-permute-done | bytes 524320 | tf_op jit(solution)/shard_map/ppermute | solution.py:59
  630.4 12.8 %shard_map.227 = (f32[512,512]{1,0:T(8,128)}, f32[512,512]{1,0:T(8,128)}, bf16[512,512]{1,0:T(8,128)(2,1)}, f32[2,512]{1,0:T(2,128)}, f32[2,512]{1,0:T(2,128)}) custom-call(f32[512,1536]{1,0:T(8,128)} %copy-done, f32[512,1536]{1,0:T(8,128)} %copy-done, f32[512,1536]{1,0:T(8,128)} %copy-done, f32[2,512]{1,0:T(2,128)} %copy-done.70, ...), custom_call_target="tpu_custom_call" | custom-call | flops 1610612736 | bytes 6291456 | tf_op jit(solution)/shard_map/pallas_call | solution.py:649
  726.9 13.0 %collective-permute-done.56.refs_7_ = bf16[128,3072]{1,0:T(8,128)(2,1)} collective-permute-done((bf16[128,3072]{1,0:T(8,128)(2,1)}, bf16[128,3072]{1,0:T(8,128)(2,1)}, u32[]{:S(2)}, u32[]{:S(2)}) %collective-permute-start.56) | collective-permute-done | bytes 786464 | tf_op jit(solution)/shard_map/ppermute | solution.py:59
  741.4 13.2 %collective-permute-done.53.refs_4_ = bf16[128,3072]{1,0:T(8,128)(2,1)} collective-permute-done((bf16[128,3072]{1,0:T(8,128)(2,1)}, bf16[128,3072]{1,0:T(8,128)(2,1)}, u32[]{:S(2)}, u32[]{:S(2)}) %collective-permute-start.53) | collective-permute-done | bytes 786464 | tf_op jit(solution)/shard_map/ppermute | solution.py:59
  755.9 17.7 %collective-permute-done.54.refs_5_ = bf16[128,3072]{1,0:T(8,128)(2,1)} collective-permute-done((bf16[128,3072]{1,0:T(8,128)(2,1)}, bf16[128,3072]{1,0:T(8,128)(2,1)}, u32[]{:S(2)}, u32[]{:S(2)}) %collective-permute-start.54) | collective-permute-done | bytes 786464 | tf_op jit(solution)/shard_map/ppermute | solution.py:59
  807.4 17.0 %collective-permute-done.48.refs_5_ = bf16[128,3072]{1,0:T(8,128)(2,1)} collective-permute-done((bf16[128,3072]{1,0:T(8,128)(2,1)}, bf16[128,3072]{1,0:T(8,128)(2,1)}, u32[]{:S(2)}, u32[]{:S(2)}) %collective-permute-start.48) | collective-permute-done | bytes 786464 | tf_op jit(solution)/shard_map/ppermute | solution.py:59
  861.5 11.7 %collective-permute-done.41 = bf16[128,2048]{1,0:T(8,128)(2,1)S(1)} collective-permute-done((bf16[128,2048]{1,0:T(8,128)(2,1)}, bf16[128,2048]{1,0:T(8,128)(2,1)S(1)}, u32[]{:S(2)}, u32[]{:S(2)}) %collective-permute-start.41) | collective-permute-done | bytes 524320 | tf_op jit(solution)/shard_map/ppermute | solution.py:59
  883.6 12.2 %all-to-all-done.1 = f32[32,24,128]{2,1,0:T(8,128)S(1)} async-done(((f32[32,24,128]{2,1,0:T(8,128)}), f32[32,24,128]{2,1,0:T(8,128)S(1)}, u32[]{:S(2)}, u32[]{:S(2)}) %all-to-all-start.1) | async-done | bytes 393248 | tf_op jit(solution)/shard_map/all_to_all | solution.py:925
  (490 shorter events, 450.9 us)
Async XLA Ops:
  7.2 86.6 %all-gather.7.cloned.1.call-start = ((), (), s32[]{:S(2)}) async-start(), calls=%async_computation.8 | async-start | bytes 7077888 | tf_op jit(solution)/shard_map/all_gather | solution.py:723
  29.1 94.1 %all-gather.9.cloned.1.call-start = ((), (), s32[]{:S(2)}) async-start(), calls=%async_computation.9 | async-start | bytes 2359296 | tf_op jit(solution)/shard_map/all_gather | solution.py:724
  29.9 305.7 %all-gather.13.cloned.1.call-start = ((), (), s32[]{:S(2)}) async-start(), calls=%async_computation.15 | async-start | bytes 4718592 | tf_op jit(solution)/shard_map/all_gather | solution.py:796
  30.6 320.6 %all-gather.11.cloned.1.call-start = ((), (), s32[]{:S(2)}) async-start(), calls=%async_computation.10 | async-start | bytes 4718592 | tf_op jit(solution)/shard_map/all_gather | solution.py:828
  156.7 436.6 %reduce-scatter.5.cloned.1.call-start = ((), (), s32[]{:S(2)}) async-start(), calls=%async_computation.11 | async-start | bytes 5013504 | tf_op jit(solution)/shard_map/reduce_scatter | solution.py:839
  191.9 128.6 %collective-permute-start.9 = (bf16[256,3072]{1,0:T(8,128)(2,1)}, bf16[256,3072]{1,0:T(8,128)(2,1)S(1)}, u32[]{:S(2)}, u32[]{:S(2)}) collective-permute-start(bf16[256,3072]{1,0:T(8,128)(2,1)} %get-tuple-element.90), channel_id=1, source_target_pairs={{0,8},{8,0},{16,24},{24,16},{1,9},{9,1},{17,25},{25,17},{2,10},{10... | collective-permute-start | bytes 4718600 | tf_op jit(solution)/shard_map/ppermute | solution.py:59
  201.1 119.4 %collective-permute-start.10 = (bf16[256,3072]{1,0:T(8,128)(2,1)}, bf16[256,3072]{1,0:T(8,128)(2,1)S(1)}, u32[]{:S(2)}, u32[]{:S(2)}) collective-permute-start(bf16[256,3072]{1,0:T(8,128)(2,1)} %get-tuple-element.91), channel_id=1, source_target_pairs={{0,16},{8,24},{16,0},{24,8},{1,17},{9,25},{17,1},{25,9},{2,18},{10... | collective-permute-start | bytes 4718600 | tf_op jit(solution)/shard_map/ppermute | solution.py:59
  209.6 110.9 %collective-permute-start.11 = (bf16[256,3072]{1,0:T(8,128)(2,1)}, bf16[256,3072]{1,0:T(8,128)(2,1)}, u32[]{:S(2)}, u32[]{:S(2)}) collective-permute-start(bf16[256,3072]{1,0:T(8,128)(2,1)} %get-tuple-element.92), channel_id=1, source_target_pairs={{0,8},{8,0},{16,24},{24,16},{1,9},{9,1},{17,25},{25,17},{2,10},{10... | collective-permute-start | bytes 4718600 | tf_op jit(solution)/shard_map/ppermute | solution.py:59
  218.0 102.5 %collective-permute-start.12 = (bf16[256,3072]{1,0:T(8,128)(2,1)}, bf16[256,3072]{1,0:T(8,128)(2,1)}, u32[]{:S(2)}, u32[]{:S(2)}) collective-permute-start(bf16[256,3072]{1,0:T(8,128)(2,1)} %get-tuple-element.93), channel_id=1, source_target_pairs={{0,16},{8,24},{16,0},{24,8},{1,17},{9,25},{17,1},{25,9},{2,18},{10... | collective-permute-start | bytes 4718600 | tf_op jit(solution)/shard_map/ppermute | solution.py:59
  226.4 73.1 %collective-permute-start.15 = (bf16[64,3072]{1,0:T(8,128)(2,1)S(1)}, bf16[64,3072]{1,0:T(8,128)(2,1)S(1)}, u32[]{:S(2)}, u32[]{:S(2)}) collective-permute-start(bf16[64,3072]{1,0:T(8,128)(2,1)S(1)} %get-tuple-element.174), channel_id=1, source_target_pairs={{0,24},{8,16},{16,8},{24,0},{1,25},{9,17},{17,9},{25,1},{2,26},{10... | collective-permute-start | bytes 1179656 | tf_op jit(solution)/shard_map/ppermute | solution.py:59
  340.4 145.5 %collective-permute-start.22 = (bf16[272,2048]{1,0:T(8,128)(2,1)}, bf16[272,2048]{1,0:T(8,128)(2,1)}, u32[]{:S(2)}, u32[]{:S(2)}) collective-permute-start(bf16[272,2048]{1,0:T(8,128)(2,1)} %fusion.14), channel_id=1, source_target_pairs={{0,8},{8,0},{16,24},{24,16},{1,9},{9,1},{17,25},{25,17},{2,10},{10... | collective-permute-start | bytes 3342344 | tf_op jit(solution)/shard_map/ppermute | solution.py:59
  347.3 87.4 %collective-permute-start.25 = (bf16[272,2048]{1,0:T(8,128)(2,1)}, bf16[272,2048]{1,0:T(8,128)(2,1)S(1)}, u32[]{:S(2)}, u32[]{:S(2)}) collective-permute-start(bf16[272,2048]{1,0:T(8,128)(2,1)} %fusion.17), channel_id=1, source_target_pairs={{0,16},{8,24},{16,0},{24,8},{1,17},{9,25},{17,1},{25,9},{2,18},{10... | collective-permute-start | bytes 3342344 | tf_op jit(solution)/shard_map/ppermute | solution.py:59
  354.9 111.9 %collective-permute-start.24 = (bf16[272,2048]{1,0:T(8,128)(2,1)S(1)}, bf16[272,2048]{1,0:T(8,128)(2,1)S(1)}, u32[]{:S(2)}, u32[]{:S(2)}) collective-permute-start(bf16[272,2048]{1,0:T(8,128)(2,1)S(1)} %convolution_convert_fusion.3), channel_id=1, source_target_pairs={{0,16},{8,24},{16,0},{24,8},{1,17},{9,25},{17,1},{25,9},{2,18},{10... | collective-permute-start | bytes 3342344 | tf_op jit(solution)/shard_map/ppermute | solution.py:59
  357.9 57.9 %collective-permute-start.27 = (bf16[272,2048]{1,0:T(8,128)(2,1)}, bf16[272,2048]{1,0:T(8,128)(2,1)S(1)}, u32[]{:S(2)}, u32[]{:S(2)}) collective-permute-start(bf16[272,2048]{1,0:T(8,128)(2,1)} %convolution_convert_fusion.2), channel_id=1, source_target_pairs={{0,24},{8,16},{16,8},{24,0},{1,25},{9,17},{17,9},{25,1},{2,26},{10... | collective-permute-start | bytes 3342344 | tf_op jit(solution)/shard_map/ppermute | solution.py:59
  392.0 93.9 %collective-permute-start.21 = (bf16[272,2048]{1,0:T(8,128)(2,1)}, bf16[272,2048]{1,0:T(8,128)(2,1)S(1)}, u32[]{:S(2)}, u32[]{:S(2)}) collective-permute-start(bf16[272,2048]{1,0:T(8,128)(2,1)} %convolution_convert_fusion.4), channel_id=1, source_target_pairs={{0,8},{8,0},{16,24},{24,16},{1,9},{9,1},{17,25},{25,17},{2,10},{10... | collective-permute-start | bytes 3342344 | tf_op jit(solution)/shard_map/ppermute | solution.py:59
  432.5 73.5 %collective-permute-start.29 = (bf16[272,2176]{1,0:T(8,128)(2,1)}, bf16[272,2176]{1,0:T(8,128)(2,1)S(1)}, u32[]{:S(2)}, u32[]{:S(2)}) collective-permute-start(bf16[272,2176]{1,0:T(8,128)(2,1)} %get-tuple-element.107), channel_id=1, source_target_pairs={{0,24},{8,16},{16,8},{24,0},{1,25},{9,17},{17,9},{25,1},{2,26},{10... | collective-permute-start | bytes 3551240 | tf_op jit(solution)/shard_map/ppermute | solution.py:59
  537.4 312.6 %reduce-scatter.7.cloned.1.call-start = ((), (), s32[]{:S(2)}) async-start(), calls=%async_computation.12 | async-start | bytes 4718592 | tf_op jit(solution)/shard_map/reduce_scatter | solution.py:862
  591.7 305.1 %reduce-scatter.9.cloned.1.call-start = ((), (), s32[]{:S(2)}) async-start(), calls=%async_computation.13 | async-start | bytes 7077888 | tf_op jit(solution)/shard_map/reduce_scatter | solution.py:901
  698.4 56.2 %collective-permute-start.53 = (bf16[128,3072]{1,0:T(8,128)(2,1)}, bf16[128,3072]{1,0:T(8,128)(2,1)}, u32[]{:S(2)}, u32[]{:S(2)}) collective-permute-start(bf16[128,3072]{1,0:T(8,128)(2,1)} %get-tuple-element.152), channel_id=1, source_target_pairs={{0,16},{8,24},{16,0},{24,8},{1,17},{9,25},{17,1},{25,9},{2,18},{10... | collective-permute-start | bytes 2359304 | tf_op jit(solution)/shard_map/ppermute | solution.py:59
  699.8 73.8 %collective-permute-start.54 = (bf16[128,3072]{1,0:T(8,128)(2,1)}, bf16[128,3072]{1,0:T(8,128)(2,1)}, u32[]{:S(2)}, u32[]{:S(2)}) collective-permute-start(bf16[128,3072]{1,0:T(8,128)(2,1)} %get-tuple-element.153), channel_id=1, source_target_pairs={{0,16},{8,24},{16,0},{24,8},{1,17},{9,25},{17,1},{25,9},{2,18},{10... | collective-permute-start | bytes 2359304 | tf_op jit(solution)/shard_map/ppermute | solution.py:59
  710.9 64.2 %collective-permute-start.51 = (bf16[128,3072]{1,0:T(8,128)(2,1)}, bf16[128,3072]{1,0:T(8,128)(2,1)}, u32[]{:S(2)}, u32[]{:S(2)}) collective-permute-start(bf16[128,3072]{1,0:T(8,128)(2,1)} %get-tuple-element.150), channel_id=1, source_target_pairs={{0,8},{8,0},{16,24},{24,16},{1,9},{9,1},{17,25},{25,17},{2,10},{10... | collective-permute-start | bytes 2359304 | tf_op jit(solution)/shard_map/ppermute | solution.py:59
  739.9 65.2 %collective-permute-start.50 = (bf16[128,3072]{1,0:T(8,128)(2,1)}, bf16[128,3072]{1,0:T(8,128)(2,1)}, u32[]{:S(2)}, u32[]{:S(2)}) collective-permute-start(bf16[128,3072]{1,0:T(8,128)(2,1)} %get-tuple-element.147), channel_id=1, source_target_pairs={{0,24},{8,16},{16,8},{24,0},{1,25},{9,17},{17,9},{25,1},{2,26},{10... | collective-permute-start | bytes 2359304 | tf_op jit(solution)/shard_map/ppermute | solution.py:59
  754.6 52.8 %collective-permute-start.47 = (bf16[128,3072]{1,0:T(8,128)(2,1)}, bf16[128,3072]{1,0:T(8,128)(2,1)}, u32[]{:S(2)}, u32[]{:S(2)}) collective-permute-start(bf16[128,3072]{1,0:T(8,128)(2,1)} %get-tuple-element.144), channel_id=1, source_target_pairs={{0,16},{8,24},{16,0},{24,8},{1,17},{9,25},{17,1},{25,9},{2,18},{10... | collective-permute-start | bytes 2359304 | tf_op jit(solution)/shard_map/ppermute | solution.py:59
  836.7 65.6 %reduce-scatter.11.cloned.1.call-start = ((), (), s32[]{:S(2)}) async-start(), calls=%async_computation.14 | async-start | bytes 2359296 | tf_op jit(solution)/shard_map/reduce_scatter | solution.py:891
  (171 other events, 1990.6 us)
Sparse Core Ops, SparseCore 0:
  29.2 64.5 all-gather.6
  95.4 27.7 all-gather.8
  124.8 46.2 all-gather.12
  173.2 45.6 all-gather.10
  537.5 51.1 reduce-scatter.4
  591.8 49.0 reduce-scatter.6
  668.0 68.8 reduce-scatter.8
  839.8 37.4 reduce-scatter.10

commit v3 on v2

--- a/solution.py
+++ b/solution.py
@@ -462,6 +462,138 @@
     return query, key, weights / jnp.sum(weights, -1, keepdims=True)
 
 
+def project_kernel(place_ref, x_ref, w_ref, out_ref, square_ref):
+    step = pl.program_id(0)
+    part = dot_nn(x_ref[...], w_ref[...])
+
+    @pl.when(step == 0)
+    def _():
+        out_ref[...] = part
+
+    @pl.when(step > 0)
+    def _():
+        out_ref[...] += part
+
+    @pl.when(step == pl.num_programs(0) - 1)
+    def _():
+        width = out_ref.shape[1] // 3
+        for n in range(2):
+            raw = out_ref[:, n * width : (n + 1) * width]
+            square_ref[n : n + 1, :] = as_row(jnp.sum(raw * raw, -1, keepdims=True))
+
+
+def project(place, x, w, total):
+    seq, width = x.shape[0], x.shape[1] // total
+    columns = w.shape[1] // total
+    return pl.pallas_call(
+        project_kernel,
+        grid_spec=pltpu.PrefetchScalarGridSpec(
+            num_scalar_prefetch=1,
+            grid=(total,),
+            in_specs=[
+                pl.BlockSpec((seq, width), lambda j, s: (0, s[0] ^ j)),
+                pl.BlockSpec((width, columns), lambda j, s: (0, j)),
+            ],
+            out_specs=[
+                pl.BlockSpec((seq, columns), lambda j, s: (0, 0)),
+                pl.BlockSpec((2, seq), lambda j, s: (0, 0)),
+            ],
+        ),
+        out_shape=[
+            jax.ShapeDtypeStruct((seq, columns), f32),
+            jax.ShapeDtypeStruct((2, seq), f32),
+        ],
+        compiler_params=pltpu.CompilerParams(vmem_limit_bytes=48 << 20),
+        cost_estimate=pl.CostEstimate(
+            flops=2 * seq * x.shape[1] * columns,
+            bytes_accessed=2 * x.size + 2 * w.size + 4 * seq * columns,
+            transcendentals=0,
+        ),
+    )(place, x, w)
+
+
+def project_back_kernel(place_ref, grad_ref, w_ref, out_ref):
+    out_ref[...] = mm_nt(grad_ref[...], w_ref[...])
+
+
+def project_back(place, grad, w, total):
+    seq, columns = grad.shape
+    width = w.shape[0]
+    return pl.pallas_call(
+        project_back_kernel,
+        grid_spec=pltpu.PrefetchScalarGridSpec(
+            num_scalar_prefetch=1,
+            grid=(total,),
+            in_specs=[
+                pl.BlockSpec((seq, columns), lambda j, s: (0, 0)),
+                pl.BlockSpec((width, columns), lambda j, s: (0, j)),
+            ],
+            out_specs=pl.BlockSpec((seq, width), lambda j, s: (0, s[0] ^ j)),
+        ),
+        out_shape=jax.ShapeDtypeStruct((seq, total * width), f32),
+        compiler_params=pltpu.CompilerParams(vmem_limit_bytes=48 << 20),
+        cost_estimate=pl.CostEstimate(
+            flops=2 * seq * w.size,
+            bytes_accessed=2 * grad.size + 2 * w.size + 4 * seq * total * width,
+            transcendentals=0,
+        ),
+    )(place, grad, w)
+
+
+def output_grad_kernel(x_ref, grad_ref, out_ref):
+    out_ref[...] = mm_tn(x_ref[...], grad_ref[...]).astype(bf16)
+
+
+def output_grad(x, grad, total):
+    seq, width = x.shape
+    return pl.pallas_call(
+        output_grad_kernel,
+        grid=(total,),
+        in_specs=[
+            pl.BlockSpec((seq, width), lambda j: (0, 0)),
+            pl.BlockSpec((seq, width), lambda j: (0, j)),
+        ],
+        out_specs=pl.BlockSpec((width, width), lambda j: (0, 3 * total + j)),
+        out_shape=jax.ShapeDtypeStruct((width, 4 * total * width), bf16),
+        compiler_params=pltpu.CompilerParams(vmem_limit_bytes=48 << 20),
+        cost_estimate=pl.CostEstimate(
+            flops=2 * seq * total * width * width,
+            bytes_accessed=4 * seq * total * width,
+            transcendentals=0,
+        ),
+    )(x, grad)
+
+
+def project_grad_kernel(place_ref, x_ref, grad_ref, held_ref, out_ref):
+    out_ref[...] = mm_tn(x_ref[...], grad_ref[...]).astype(bf16)
+
+
+def project_grad(place, x, grad, held, total):
+    seq, columns = grad.shape
+    width = x.shape[1] // total
+    return pl.pallas_call(
+        project_grad_kernel,
+        grid_spec=pltpu.PrefetchScalarGridSpec(
+            num_scalar_prefetch=1,
+            grid=(total,),
+            in_specs=[
+                pl.BlockSpec((seq, width), lambda j, s: (0, s[0] ^ j)),
+                pl.BlockSpec((seq, columns), lambda j, s: (0, 0)),
+                pl.BlockSpec(memory_space=pl.ANY),
+            ],
+            out_specs=pl.BlockSpec((width, columns), lambda j, s: (0, j)),
+        ),
+        out_shape=jax.ShapeDtypeStruct(held.shape, bf16),
+        input_output_aliases={3: 0},
+        compiler_params=pltpu.CompilerParams(vmem_limit_bytes=48 << 20),
+        cost_estimate=pl.CostEstimate(
+            flops=2 * seq * x.shape[1] * columns,
+            bytes_accessed=2 * x.size + 2 * grad.size + 2 * total * width * columns,
+            transcendentals=0,
+        ),
+    )(place, x, grad, held)
+
+
 def attend_kernel(model_width, q_ref, k_ref, v_ref, gain_ref, cos_ref, sin_ref, rp, cp, *refs):
     parts, out_ref, scale_ref = refs[:-2], refs[-2], refs[-1]
 
@@ -696,7 +828,6 @@
     devices = C * F
     W = model_width // C
     seq = C * row_total
-    shard = w_query.shape[0]
     pieces = C // local_experts
     cap_unit = 16 * expert_total * pieces
     piece_cap = (17 * row_total * top_count + cap_unit - 1) // cap_unit
@@ -710,17 +841,17 @@
     route_ids = routes.reshape(row_total, top_count)
     column_ids = lax.all_gather(route_ids, FSDP, axis=0, tiled=True)
 
-    def by_column(weight):
-        return jnp.swapaxes(weight.reshape(shard, C, W), 0, 1)
-
-    w_cols = lax.all_to_all(
-        jnp.concatenate([by_column(w_query), by_column(w_key), by_column(w_value)], 2),
-        CTX,
-        split_axis=0,
-        concat_axis=0,
-        tiled=True,
-    )
-    w_qkv = lax.all_gather(w_cols, FSDP, axis=1, tiled=True).reshape(model_width, 3 * W)
+    blocks = []
+    for j in range(C):
+        piece = jnp.concatenate(
+            [
+                lax.dynamic_slice_in_dim(w, (me ^ j) * W, W, 1)
+                for w in (w_query, w_key, w_value)
+            ],
+            1,
+        )
+        blocks.append(from_peer(piece, j, C) if j else piece)
+    w_qkv = lax.all_gather(jnp.concatenate(blocks, 1), FSDP, axis=0, tiled=True)
     w_o = lax.all_gather(output_weight, FSDP, axis=0, tiled=True)
 
     by_expert = lax.optimization_barrier(
@@ -812,10 +943,9 @@
     gains = lax.dynamic_slice_in_dim(jnp.stack([query_gain, key_gain]), my_column, W, 1)
     places = jnp.concatenate(places, 1)
     w_qkv, selects, places = lax.optimization_barrier((w_qkv, selects, places))
-    raw_qkv = mm(normed, w_qkv)
-    raw_q = raw_qkv[:, :W]
-    raw_k = raw_qkv[:, W : 2 * W]
-    squares = spread_rows(jnp.stack([jnp.sum(raw_q * raw_q, -1), jnp.sum(raw_k * raw_k, -1)]), C)
+    place = me.reshape(1)
+    raw_qkv, squares = project(place, normed, w_qkv, C)
+    squares = spread_rows(squares, C)
     signed_sine = jnp.where(jnp.arange(HD) < HD // 2, -1.0, 1.0) * sine
     tables = (gains, cosine, signed_sine, positions.reshape(seq, 1), positions.reshape(1, seq))
     attended, scales = attend(raw_qkv, tables, squares, model_width)
@@ -885,10 +1015,7 @@
 
     branch_seq = gather_rows(grad_hidden_one.astype(bf16), C)
     grad_att = mm_nt(branch_seq, w_o).astype(bf16)
-    d_output = mm_tn(attended, branch_seq).astype(bf16)
-    grad_att, d_output = lax.optimization_barrier((grad_att, d_output))
-
-    d_output = lax.psum_scatter(d_output, FSDP, scatter_dimension=0, tiled=True).astype(f32)
+    weight_sums = output_grad(attended, branch_seq, C)
     grad_q_n, grad_k_n, grad_value, dots, gain_grads = attend_back(
         raw_qkv, tables, scales, grad_att
     )
@@ -898,15 +1025,17 @@
     grad_qkv = finish(
         model_width, grad_q_n, grad_k_n, grad_value, raw_qkv, gains, scales, dots
     )
-    d_cols = lax.psum_scatter(
-        mm_tn(normed, grad_qkv).astype(bf16).reshape(C, F * shard, 3 * W),
+    weight_sums = lax.psum_scatter(
+        project_grad(place, normed, grad_qkv, weight_sums, C),
         FSDP,
-        scatter_dimension=1,
+        scatter_dimension=0,
         tiled=True,
     )
+    d_cols = weight_sums[:, : 3 * model_width]
+    d_output = weight_sums[:, 3 * model_width :].astype(f32)
     received = []
     for j in range(C):
-        piece = lax.dynamic_index_in_dim(d_cols, me ^ j, 0, keepdims=False)
+        piece = d_cols[:, 3 * W * j : 3 * W * (j + 1)]
         received.append(from_peer(piece, j, C) if j else piece)
     received = jnp.stack(received)
     received = [
@@ -917,7 +1046,7 @@
         for n in range(3)
     ]
 
-    grad_normed = scatter_rows(mm_nt(grad_qkv, w_qkv), C)
+    grad_normed = scatter_rows(project_back(place, grad_qkv, w_qkv, C), C)
     grad_inputs, grad_attn_gain = norm_back(grad_normed, inputs, scale_one[:row_total], attn_gain)
     grad_inputs = grad_inputs + grad_hidden_one
 

time: 924 us -> 914 us (0.989)
  matrix products: 55.3 us -> 28.4 us
  Pallas kernels: 161 us -> 182 us
  blocking collectives: 31.4 us -> 14.8 us
    pallas_call x0 -> x4, Pallas kernels: none -> 22 us  [the longest x1 6.96 us: project(): pl.pallas_call(project_kernel, grid_spec=pltpu.PrefetchScalarGridSpec(num...]
    all_to_all x1 -> x0, blocking collectives: 16.5 us -> none  [layer(): lax.all_to_all(jnp.concatenate([by_column(w_query), by_column(w_key), by_...]
    dot_general x3 -> x1, matrix products: 12.3 us -> 1.47 us  [mm_tn(): lax.dot_general(a, b, (((0,), (0,)), ((), ())), preferred_element_type=f32)]
    ppermute x57 -> x60, waiting for transfers between devices: 401 us -> 411 us  [from_peer(): return lax.ppermute(values, CTX, [(i, i ^ offset) for i in range(total)])]
    dot_general x11 -> x10, matrix products: 31.2 us -> 24.1 us  [mm(): return jnp.dot(a, b, preferred_element_type=f32)]
    ppermute x57 -> x60, starting transfers between devices: 73 us -> 76.9 us  [from_peer(): return lax.ppermute(values, CTX, [(i, i ^ offset) for i in range(total)])]
    unnamed x257 -> x207, local copies, waits for them, and re-layouts: 51.8 us -> 48.2 us
  transfers between devices with their start and end apart: 68 -> 70, of which waited for: 42 -> 42; matrix products, arithmetic and copies ran while one was open for 13% -> 10% of each run, Pallas kernels for 16% -> 19%
where the time goes in v3:
time: 914 us; the launch traced here: 903 us
  waiting for transfers between devices  456 us (50%)
  Pallas kernels  182 us (20%)
  starting transfers between devices  89.5 us (10%)
  local copies, waits for them, and re-layouts  86.1 us (9%)
  other arithmetic  29.8 us (3%)
  matrix products  28.4 us (3%)
  between operations  15.7 us (2%)
  blocking collectives  14.8 us (2%)
    ppermute x60, waiting for transfers between devices, from_peer(): return lax.ppermute(values, CTX, [(i, i ^ offset) for i in range(total)])  411 us
    ppermute x60, starting transfers between devices, from_peer(): return lax.ppermute(values, CTX, [(i, i ^ offset) for i in range(total)])  76.9 us
    pallas_call x4, Pallas kernels, run_expert(): pl.pallas_call(functools.partial(expert_kernel, steps), grid_spec=pltpu.P...  56.4 us
    unnamed x207, local copies, waits for them, and re-layouts  48.2 us
    pallas_call x4, Pallas kernels, weight_grad(): pl.pallas_call(functools.partial(weight_kernel, len(groups), steps), grid...  37.6 us
    all_gather x1, waiting for transfers between devices, layer(): w_qkv = lax.all_gather(jnp.concatenate(blocks, 1), FSDP, axis=0, tiled=True)  27.5 us
    dot_general x10, matrix products, mm(): return jnp.dot(a, b, preferred_element_type=f32)  24.1 us
    pallas_call x2, Pallas kernels, collect_rows(): pl.pallas_call(functools.partial(collect_kernel, len(parts)), grid=(pl.cd...  18.9 us
  transfers between devices with their start and end apart: 70, of which 42 were waited for; matrix products, arithmetic and copies ran while one was open for 10% of the time, Pallas kernels for 19%

profile of v3, /device:TPU:0, one launch (start us, length us, event | category | flops | bytes accessed | tf_op | source)
XLA Modules:
  0.0 903.1 jit_solution(4008972127926931305)
XLA Ops:
  29.7 14.8 %all-gather = s32[1,1024,8]{1,2,0:T(8,128)S(1)} all-gather(s32[1,128,8]{1,2,0:T(8,128)S(1)} %copy-done.97), channel_id=2, replica_groups=mesh['ctx'=4,'fsdp'=8] {'fsdp'}, dimensions={1}, use_global_device_ids=true | all-gather | bytes 36864 | tf_op jit(solution)/shard_map/all_gather | solution.py:842
  63.5 27.5 %all-gather.7.cloned.1.call-done.w_ref = bf16[512,6144]{1,0:T(8,128)(2,1)} async-done(((bf16[64,6144]{1,0:T(8,128)(2,1)}), bf16[512,6144]{1,0:T(8,128)(2,1)}) %all-gather.7.cloned.1.call-update) | async-done | bytes 6291472 | tf_op jit(solution)/shard_map/all_gather | solution.py:854
  127.2 11.3 %collective-permute-done.9 = bf16[128,2048]{1,0:T(8,128)(2,1)S(1)} collective-permute-done((bf16[128,2048]{1,0:T(8,128)(2,1)S(1)}, bf16[128,2048]{1,0:T(8,128)(2,1)S(1)}, u32[]{:S(2)}, u32[]{:S(2)}) %collective-permute-start.9) | collective-permute-done | bytes 524320 | tf_op jit(solution)/shard_map/ppermute | solution.py:59
  138.5 11.5 %collective-permute-done.11 = bf16[128,2048]{1,0:T(8,128)(2,1)S(1)} collective-permute-done((bf16[128,2048]{1,0:T(8,128)(2,1)S(1)}, bf16[128,2048]{1,0:T(8,128)(2,1)S(1)}, u32[]{:S(2)}, u32[]{:S(2)}) %collective-permute-start.11) | collective-permute-done | bytes 524320 | tf_op jit(solution)/shard_map/ppermute | solution.py:59
  154.1 13.3 %copy.108 = bf16[512,4,3072]{2,0,1:T(8,128)(2,1)} copy(bf16[512,4,3072]{2,1,0:T(4,128)(2,1)} %param.23) | data formatting | bytes 25165824 | tf_op jit(solution)/shard_map/optimization_barrier | solution.py:858
  224.8 71.5 %collective-permute-done.18.refs_8_ = bf16[64,3072]{1,0:T(8,128)(2,1)S(1)} collective-permute-done((bf16[64,3072]{1,0:T(8,128)(2,1)S(1)}, bf16[64,3072]{1,0:T(8,128)(2,1)S(1)}, u32[]{:S(2)}, u32[]{:S(2)}) %collective-permute-start.18) | collective-permute-done | bytes 393248 | tf_op jit(solution)/shard_map/ppermute | solution.py:59
  356.4 14.2 %shard_map.223 = (bf16[272,2176]{1,0:T(8,128)(2,1)}, bf16[272,2048]{1,0:T(8,128)(2,1)S(1)}, bf16[272,2048]{1,0:T(8,128)(2,1)S(1)}, bf16[272,1024]{1,0:T(8,128)(2...) custom-call(s32[1]{0:T(128)} %bitcast.14.mine_ref, ...), custom_call_target="tpu_custom_call" | custom-call | flops 6845104128 | bytes 18153472 | tf_op jit(solution)/shard_map/pallas_call | solution.py:308
  372.0 15.1 %collective-permute-done.31.cots_ref = bf16[272,2048]{1,0:T(8,128)(2,1)} collective-permute-done((bf16[272,2048]{1,0:T(8,128)(2,1)}, bf16[272,2048]{1,0:T(8,128)(2,1)}, u32[]{:S(2)}, u32[]{:S(2)}) %collective-permute-start.31) | collective-permute-done | bytes 1114144 | tf_op jit(solution)/shard_map/ppermute | solution.py:59
  388.5 22.2 %collective-permute-done.30.rows_ref.refs_15_ = bf16[272,2048]{1,0:T(8,128)(2,1)S(1)} collective-permute-done((bf16[272,2048]{1,0:T(8,128)(2,1)}, bf16[272,2048]{1,0:T(8,128)(2,1)S(1)}, u32[]{:S(2)}, u32[]{:S(2)}) %collective-permute-start.30) | collective-permute-done | bytes 1114144 | tf_op jit(solution)/shard_map/ppermute | solution.py:59
  410.8 14.1 %shard_map.226 = (bf16[272,2176]{1,0:T(8,128)(2,1)}, bf16[272,2048]{1,0:T(8,128)(2,1)S(1)}, bf16[272,2048]{1,0:T(8,128)(2,1)S(1)}, bf16[272,1024]{1,0:T(8,128)(2...) custom-call(s32[1]{0:T(128)} %bitcast.14.mine_ref, ...), custom_call_target="tpu_custom_call" | custom-call | flops 6845104128 | bytes 18153472 | tf_op jit(solution)/shard_map/pallas_call | solution.py:308
  429.7 32.0 %collective-permute-done.27.rows_ref.refs_10_ = bf16[272,2048]{1,0:T(8,128)(2,1)S(1)} collective-permute-done((bf16[272,2048]{1,0:T(8,128)(2,1)S(1)}, bf16[272,2048]{1,0:T(8,128)(2,1)S(1)}, u32[]{:S(2)}, u32[]{:S(2)}) %collective-permute-start.27) | collective-permute-done | bytes 1114144 | tf_op jit(solution)/shard_map/ppermute | solution.py:59
  461.7 14.1 %shard_map.225 = (bf16[272,2176]{1,0:T(8,128)(2,1)}, bf16[272,2048]{1,0:T(8,128)(2,1)S(1)}, bf16[272,2048]{1,0:T(8,128)(2,1)S(1)}, bf16[272,1024]{1,0:T(8,128)(2...) custom-call(s32[1]{0:T(128)} %bitcast.14.mine_ref, ...), custom_call_target="tpu_custom_call" | custom-call | flops 6845104128 | bytes 18153472 | tf_op jit(solution)/shard_map/pallas_call | solution.py:308
  480.9 14.1 %shard_map.224 = (bf16[272,2176]{1,0:T(8,128)(2,1)}, bf16[272,2048]{1,0:T(8,128)(2,1)S(1)}, bf16[272,2048]{1,0:T(8,128)(2,1)S(1)}, bf16[272,1024]{1,0:T(8,128)(2...) custom-call(s32[1]{0:T(128)} %bitcast.14.mine_ref, ...), custom_call_target="tpu_custom_call" | custom-call | flops 6845104128 | bytes 18153472 | tf_op jit(solution)/shard_map/pallas_call | solution.py:308
  501.5 19.9 %collective-permute-done.26.refs_2_ = bf16[272,2176]{1,0:T(8,128)(2,1)S(1)} collective-permute-done((bf16[272,2176]{1,0:T(8,128)(2,1)}, bf16[272,2176]{1,0:T(8,128)(2,1)S(1)}, u32[]{:S(2)}, u32[]{:S(2)}) %collective-permute-start.26) | collective-permute-done | bytes 1183776 | tf_op jit(solution)/shard_map/ppermute | solution.py:59
  534.9 25.1 %collective-permute-done.41.refs_4_ = bf16[272,2048]{1,0:T(8,128)(2,1)S(1)} collective-permute-done((bf16[272,2048]{1,0:T(8,128)(2,1)}, bf16[272,2048]{1,0:T(8,128)(2,1)S(1)}, u32[]{:S(2)}, u32[]{:S(2)}) %collective-permute-start.41) | collective-permute-done | bytes 1114144 | tf_op jit(solution)/shard_map/ppermute | solution.py:59
  559.9 16.6 %collective-permute-done.40.refs_3_ = bf16[272,2048]{1,0:T(8,128)(2,1)S(1)} collective-permute-done((bf16[272,2048]{1,0:T(8,128)(2,1)}, bf16[272,2048]{1,0:T(8,128)(2,1)S(1)}, u32[]{:S(2)}, u32[]{:S(2)}) %collective-permute-start.40) | collective-permute-done | bytes 1114144 | tf_op jit(solution)/shard_map/ppermute | solution.py:59
  594.4 12.2 %collective-permute-done.35 = bf16[128,2048]{1,0:T(8,128)(2,1)S(1)} collective-permute-done((bf16[128,2048]{1,0:T(8,128)(2,1)S(1)}, bf16[128,2048]{1,0:T(8,128)(2,1)S(1)}, u32[]{:S(2)}, u32[]{:S(2)}) %collective-permute-start.35) | collective-permute-done | bytes 524320 | tf_op jit(solution)/shard_map/ppermute | solution.py:59
  619.1 12.7 %shard_map.228 = (f32[512,512]{1,0:T(8,128)}, f32[512,512]{1,0:T(8,128)}, bf16[512,512]{1,0:T(8,128)(2,1)}, f32[2,512]{1,0:T(2,128)}, f32[2,512]{1,0:T(2,128)}) custom-call(f32[512,1536]{1,0:T(8,128)} %copy-done, f32[512,1536]{1,0:T(8,128)} %copy-done, f32[512,1536]{1,0:T(8,128)} %copy-done, f32[2,512]{1,0:T(2,128)} %copy-done.63, ...), custom_call_target="tpu_custom_call" | custom-call | flops 1610612736 | bytes 6291456 | tf_op jit(solution)/shard_map/pallas_call | solution.py:781
  711.2 13.1 %collective-permute-done.59.refs_7_ = bf16[128,3072]{1,0:T(8,128)(2,1)} collective-permute-done((bf16[128,3072]{1,0:T(8,128)(2,1)}, bf16[128,3072]{1,0:T(8,128)(2,1)}, u32[]{:S(2)}, u32[]{:S(2)}) %collective-permute-start.59) | collective-permute-done | bytes 786464 | tf_op jit(solution)/shard_map/ppermute | solution.py:59
  725.7 13.7 %collective-permute-done.56.refs_4_ = bf16[128,3072]{1,0:T(8,128)(2,1)} collective-permute-done((bf16[128,3072]{1,0:T(8,128)(2,1)}, bf16[128,3072]{1,0:T(8,128)(2,1)}, u32[]{:S(2)}, u32[]{:S(2)}) %collective-permute-start.56) | collective-permute-done | bytes 786464 | tf_op jit(solution)/shard_map/ppermute | solution.py:59
  740.9 17.2 %collective-permute-done.57.refs_5_ = bf16[128,3072]{1,0:T(8,128)(2,1)} collective-permute-done((bf16[128,3072]{1,0:T(8,128)(2,1)}, bf16[128,3072]{1,0:T(8,128)(2,1)}, u32[]{:S(2)}, u32[]{:S(2)}) %collective-permute-start.57) | collective-permute-done | bytes 786464 | tf_op jit(solution)/shard_map/ppermute | solution.py:59
  792.9 16.3 %collective-permute-done.51.refs_5_ = bf16[128,3072]{1,0:T(8,128)(2,1)} collective-permute-done((bf16[128,3072]{1,0:T(8,128)(2,1)}, bf16[128,3072]{1,0:T(8,128)(2,1)}, u32[]{:S(2)}, u32[]{:S(2)}) %collective-permute-start.51) | collective-permute-done | bytes 786464 | tf_op jit(solution)/shard_map/ppermute | solution.py:59
  844.7 11.8 %collective-permute-done.44 = bf16[128,2048]{1,0:T(8,128)(2,1)} collective-permute-done((bf16[128,2048]{1,0:T(8,128)(2,1)}, bf16[128,2048]{1,0:T(8,128)(2,1)}, u32[]{:S(2)}, u32[]{:S(2)}) %collective-permute-start.44) | collective-permute-done | bytes 524320 | tf_op jit(solution)/shard_map/ppermute | solution.py:59
  866.8 12.2 %all-to-all-done = f32[32,24,128]{2,1,0:T(8,128)S(1)} async-done(((f32[32,24,128]{2,1,0:T(8,128)}), f32[32,24,128]{2,1,0:T(8,128)S(1)}, u32[]{:S(2)}, u32[]{:S(2)}) %all-to-all-start) | async-done | bytes 393248 | tf_op jit(solution)/shard_map/all_to_all | solution.py:1054
  (443 shorter events, 441.0 us)
Async XLA Ops:
  7.2 83.8 %all-gather.7.cloned.1.call-start = ((), (), s32[]{:S(2)}) async-start(), calls=%async_computation.6 | async-start | bytes 7077888 | tf_op jit(solution)/shard_map/all_gather | solution.py:854
  24.6 95.9 %all-gather.9.cloned.1.call-start = ((), (), s32[]{:S(2)}) async-start(), calls=%async_computation.7 | async-start | bytes 2359296 | tf_op jit(solution)/shard_map/all_gather | solution.py:855
  25.3 305.2 %all-gather.13.cloned.1.call-start = ((), (), s32[]{:S(2)}) async-start(), calls=%async_computation.12 | async-start | bytes 4718592 | tf_op jit(solution)/shard_map/all_gather | solution.py:927
  26.1 320.0 %all-gather.11.cloned.1.call-start = ((), (), s32[]{:S(2)}) async-start(), calls=%async_computation.8 | async-start | bytes 4718592 | tf_op jit(solution)/shard_map/all_gather | solution.py:958
  153.9 433.6 %reduce-scatter.4.cloned.1.call-start = ((), (), s32[]{:S(2)}) async-start(), calls=%async_computation.9 | async-start | bytes 5013504 | tf_op jit(solution)/shard_map/reduce_scatter | solution.py:969
  188.9 128.2 %collective-permute-start.12 = (bf16[256,3072]{1,0:T(8,128)(2,1)}, bf16[256,3072]{1,0:T(8,128)(2,1)S(1)}, u32[]{:S(2)}, u32[]{:S(2)}) collective-permute-start(bf16[256,3072]{1,0:T(8,128)(2,1)} %get-tuple-element.92), channel_id=1, source_target_pairs={{0,8},{8,0},{16,24},{24,16},{1,9},{9,1},{17,25},{25,17},{2,10},{10... | collective-permute-start | bytes 4718600 | tf_op jit(solution)/shard_map/ppermute | solution.py:59
  197.4 119.7 %collective-permute-start.13 = (bf16[256,3072]{1,0:T(8,128)(2,1)}, bf16[256,3072]{1,0:T(8,128)(2,1)}, u32[]{:S(2)}, u32[]{:S(2)}) collective-permute-start(bf16[256,3072]{1,0:T(8,128)(2,1)} %get-tuple-element.93), channel_id=1, source_target_pairs={{0,16},{8,24},{16,0},{24,8},{1,17},{9,25},{17,1},{25,9},{2,18},{10... | collective-permute-start | bytes 4718600 | tf_op jit(solution)/shard_map/ppermute | solution.py:59
  205.9 111.3 %collective-permute-start.14 = (bf16[256,3072]{1,0:T(8,128)(2,1)}, bf16[256,3072]{1,0:T(8,128)(2,1)}, u32[]{:S(2)}, u32[]{:S(2)}) collective-permute-start(bf16[256,3072]{1,0:T(8,128)(2,1)} %get-tuple-element.94), channel_id=1, source_target_pairs={{0,8},{8,0},{16,24},{24,16},{1,9},{9,1},{17,25},{25,17},{2,10},{10... | collective-permute-start | bytes 4718600 | tf_op jit(solution)/shard_map/ppermute | solution.py:59
  215.1 102.1 %collective-permute-start.15 = (bf16[256,3072]{1,0:T(8,128)(2,1)}, bf16[256,3072]{1,0:T(8,128)(2,1)}, u32[]{:S(2)}, u32[]{:S(2)}) collective-permute-start(bf16[256,3072]{1,0:T(8,128)(2,1)} %get-tuple-element.95), channel_id=1, source_target_pairs={{0,16},{8,24},{16,0},{24,8},{1,17},{9,25},{17,1},{25,9},{2,18},{10... | collective-permute-start | bytes 4718600 | tf_op jit(solution)/shard_map/ppermute | solution.py:59
  223.4 73.0 %collective-permute-start.18 = (bf16[64,3072]{1,0:T(8,128)(2,1)S(1)}, bf16[64,3072]{1,0:T(8,128)(2,1)S(1)}, u32[]{:S(2)}, u32[]{:S(2)}) collective-permute-start(bf16[64,3072]{1,0:T(8,128)(2,1)S(1)} %get-tuple-element.172), channel_id=1, source_target_pairs={{0,24},{8,16},{16,8},{24,0},{1,25},{9,17},{17,9},{25,1},{2,26},{10... | collective-permute-start | bytes 1179656 | tf_op jit(solution)/shard_map/ppermute | solution.py:59
  335.3 144.5 %collective-permute-start.25 = (bf16[272,2048]{1,0:T(8,128)(2,1)}, bf16[272,2048]{1,0:T(8,128)(2,1)S(1)}, u32[]{:S(2)}, u32[]{:S(2)}) collective-permute-start(bf16[272,2048]{1,0:T(8,128)(2,1)} %fusion.14), channel_id=1, source_target_pairs={{0,8},{8,0},{16,24},{24,16},{1,9},{9,1},{17,25},{25,17},{2,10},{10... | collective-permute-start | bytes 3342344 | tf_op jit(solution)/shard_map/ppermute | solution.py:59
  342.2 87.5 %collective-permute-start.28 = (bf16[272,2048]{1,0:T(8,128)(2,1)}, bf16[272,2048]{1,0:T(8,128)(2,1)}, u32[]{:S(2)}, u32[]{:S(2)}) collective-permute-start(bf16[272,2048]{1,0:T(8,128)(2,1)} %fusion.17), channel_id=1, source_target_pairs={{0,16},{8,24},{16,0},{24,8},{1,17},{9,25},{17,1},{25,9},{2,18},{10... | collective-permute-start | bytes 3342344 | tf_op jit(solution)/shard_map/ppermute | solution.py:59
  349.8 111.9 %collective-permute-start.27 = (bf16[272,2048]{1,0:T(8,128)(2,1)S(1)}, bf16[272,2048]{1,0:T(8,128)(2,1)S(1)}, u32[]{:S(2)}, u32[]{:S(2)}) collective-permute-start(bf16[272,2048]{1,0:T(8,128)(2,1)S(1)} %convolution_convert_fusion.1), channel_id=1, source_target_pairs={{0,16},{8,24},{16,0},{24,8},{1,17},{9,25},{17,1},{25,9},{2,18},{10... | collective-permute-start | bytes 3342344 | tf_op jit(solution)/shard_map/ppermute | solution.py:59
  352.8 57.9 %collective-permute-start.30 = (bf16[272,2048]{1,0:T(8,128)(2,1)}, bf16[272,2048]{1,0:T(8,128)(2,1)S(1)}, u32[]{:S(2)}, u32[]{:S(2)}) collective-permute-start(bf16[272,2048]{1,0:T(8,128)(2,1)} %convolution_convert_fusion), channel_id=1, source_target_pairs={{0,24},{8,16},{16,8},{24,0},{1,25},{9,17},{17,9},{25,1},{2,26},{10... | collective-permute-start | bytes 3342344 | tf_op jit(solution)/shard_map/ppermute | solution.py:59
  387.1 93.8 %collective-permute-start.24 = (bf16[272,2048]{1,0:T(8,128)(2,1)S(1)}, bf16[272,2048]{1,0:T(8,128)(2,1)S(1)}, u32[]{:S(2)}, u32[]{:S(2)}) collective-permute-start(bf16[272,2048]{1,0:T(8,128)(2,1)S(1)} %convolution_convert_fusion.2), channel_id=1, source_target_pairs={{0,8},{8,0},{16,24},{24,16},{1,9},{9,1},{17,25},{25,17},{2,10},{10... | collective-permute-start | bytes 3342344 | tf_op jit(solution)/shard_map/ppermute | solution.py:59
  427.5 72.5 %collective-permute-start.32 = (bf16[272,2176]{1,0:T(8,128)(2,1)}, bf16[272,2176]{1,0:T(8,128)(2,1)S(1)}, u32[]{:S(2)}, u32[]{:S(2)}) collective-permute-start(bf16[272,2176]{1,0:T(8,128)(2,1)} %get-tuple-element.109), channel_id=1, source_target_pairs={{0,24},{8,16},{16,8},{24,0},{1,25},{9,17},{17,9},{25,1},{2,26},{10... | collective-permute-start | bytes 3551240 | tf_op jit(solution)/shard_map/ppermute | solution.py:59
  531.3 302.0 %reduce-scatter.6.cloned.1.call-start = ((), (), s32[]{:S(2)}) async-start(), calls=%async_computation.10 | async-start | bytes 4718592 | tf_op jit(solution)/shard_map/reduce_scatter | solution.py:992
  585.8 294.8 %reduce-scatter.8.cloned.1.call-start = ((), (), s32[]{:S(2)}) async-start(), calls=%async_computation.11 | async-start | bytes 9437184 | tf_op jit(solution)/shard_map/reduce_scatter | solution.py:1028
  682.7 56.7 %collective-permute-start.56 = (bf16[128,3072]{1,0:T(8,128)(2,1)}, bf16[128,3072]{1,0:T(8,128)(2,1)}, u32[]{:S(2)}, u32[]{:S(2)}) collective-permute-start(bf16[128,3072]{1,0:T(8,128)(2,1)} %get-tuple-element.152), channel_id=1, source_target_pairs={{0,16},{8,24},{16,0},{24,8},{1,17},{9,25},{17,1},{25,9},{2,18},{10... | collective-permute-start | bytes 2359304 | tf_op jit(solution)/shard_map/ppermute | solution.py:59
  684.1 74.0 %collective-permute-start.57 = (bf16[128,3072]{1,0:T(8,128)(2,1)}, bf16[128,3072]{1,0:T(8,128)(2,1)}, u32[]{:S(2)}, u32[]{:S(2)}) collective-permute-start(bf16[128,3072]{1,0:T(8,128)(2,1)} %get-tuple-element.153), channel_id=1, source_target_pairs={{0,16},{8,24},{16,0},{24,8},{1,17},{9,25},{17,1},{25,9},{2,18},{10... | collective-permute-start | bytes 2359304 | tf_op jit(solution)/shard_map/ppermute | solution.py:59
  695.0 64.5 %collective-permute-start.54 = (bf16[128,3072]{1,0:T(8,128)(2,1)}, bf16[128,3072]{1,0:T(8,128)(2,1)}, u32[]{:S(2)}, u32[]{:S(2)}) collective-permute-start(bf16[128,3072]{1,0:T(8,128)(2,1)} %get-tuple-element.150), channel_id=1, source_target_pairs={{0,8},{8,0},{16,24},{24,16},{1,9},{9,1},{17,25},{25,17},{2,10},{10... | collective-permute-start | bytes 2359304 | tf_op jit(solution)/shard_map/ppermute | solution.py:59
  724.3 68.6 %collective-permute-start.53 = (bf16[128,3072]{1,0:T(8,128)(2,1)}, bf16[128,3072]{1,0:T(8,128)(2,1)}, u32[]{:S(2)}, u32[]{:S(2)}) collective-permute-start(bf16[128,3072]{1,0:T(8,128)(2,1)} %get-tuple-element.147), channel_id=1, source_target_pairs={{0,24},{8,16},{16,8},{24,0},{1,25},{9,17},{17,9},{25,1},{2,26},{10... | collective-permute-start | bytes 2359304 | tf_op jit(solution)/shard_map/ppermute | solution.py:59
  739.4 53.5 %collective-permute-start.50 = (bf16[128,3072]{1,0:T(8,128)(2,1)}, bf16[128,3072]{1,0:T(8,128)(2,1)}, u32[]{:S(2)}, u32[]{:S(2)}) collective-permute-start(bf16[128,3072]{1,0:T(8,128)(2,1)} %get-tuple-element.144), channel_id=1, source_target_pairs={{0,16},{8,24},{16,0},{24,8},{1,17},{9,25},{17,1},{25,9},{2,18},{10... | collective-permute-start | bytes 2359304 | tf_op jit(solution)/shard_map/ppermute | solution.py:59
  762.5 53.1 %all-to-all-start.1 = ((f32[32,1,2112]{2,1,0:T(1,128)}), f32[32,1,2112]{2,1,0:T(1,128)S(1)}, u32[]{:S(2)}, u32[]{:S(2)}) async-start(f32[32,1,2112]{2,1,0:T(1,128)} %copy.92), calls=%async_computation.4 | async-start | bytes 557056 | tf_op jit(solution)/shard_map/all_to_all | solution.py:1009
  (147 other events, 2029.0 us)
Sparse Core Ops, SparseCore 0:
  24.7 66.2 all-gather.6
  92.6 27.7 all-gather.8
  122.1 46.2 all-gather.12
  170.4 45.6 all-gather.10
  531.4 51.9 reduce-scatter.3
  585.9 49.2 reduce-scatter.5
  651.1 88.6 reduce-scatter.7
